TPU v7x, 32 devices: a whole 2x2x4 slice. The times are simulated.
32 devices in a mesh: scen: 2 (over x), tm: 16 (over z, y, core).
Axes of the slice: x: 2, y: 2, z: 4, core: 2. Of those that a mesh axis runs over, the one named last changes fastest.
Arguments:
- base_injection: bfloat16 [32, 36864], P(('scen', 'tm')), parts along dimension 0, may hold values from -6 to 6
- ptdf_tiles: bfloat16 [128, 80, 128, 128], P(None, 'tm'), may hold values from -0.0625 to 0.0625
- tile_block: int32 [128, 80], P(None, 'tm'), may hold values from 0 to 17
- limits: float32 [16384], replicated, may hold values from 0.5 to 2
- stor_bus: int32 [2048], replicated, may hold values from 0 to 36863
- stor_gain: float32 [2048], replicated, may hold values from 0.5 to 4
- soc_init: float32 [32, 2048], P(('scen', 'tm')), parts along dimension 0, may hold values from 0 to 1
Outputs:
- injection: float32 [32, 36864], P(('scen', 'tm')), parts along dimension 0
- line_dual: float32 [32, 16384], P(('scen', 'tm')), parts along dimension 0
- level: float32 [32, 2048], P(('scen', 'tm')), parts along dimension 0
There are 2 independent parts, one for each index of `scen`. A program takes and returns all parts, laid end to end along the dimension named above; an argument that names none is the same for every part. Nothing has to cross between parts.
All inputs are finite; a program needn't handle non-finite values.
Results may differ from a plain program's by a relative error of at most 0.012.
The roundings to bfloat16 on the way count: a program that leaves them out, or rounds other values in their place, can miss the bound.
Values may be sent and summed in bfloat16 or wider, within the bound.
A program may use at most 128 MiB of HBM per device.

v0:
```python
import jax
import jax.numpy as jnp
from jax import lax
from jax.sharding import PartitionSpec as P

ITERS = 2


step_size = 0.5
penalty = 4.0
ramp_weight = 0.5


def padded_2(block, sides, width):
    for axis, dim in sides:
        count = lax.axis_size(axis)
        forward = [(i, i + 1) for i in range(count - 1)]
        forward.append((count - 1, 0))
        backward = [(target, source) for source, target in forward]
        low = lax.ppermute(
            lax.slice_in_dim(block, block.shape[dim] - width, None, axis=dim), axis, forward
        )
        high = lax.ppermute(lax.slice_in_dim(block, 0, width, axis=dim), axis, backward)
        block = jnp.concatenate([low, block, high], axis=dim)
    return block


def shards(base_injection, ptdf_tiles, tile_block, limits, stor_bus, stor_gain, soc_init):
    hour_rows = base_injection.shape[0]
    bus_count = base_injection.shape[1]
    line_count = limits.shape[0]
    groups = ptdf_tiles.shape[0]
    tile_width = ptdf_tiles.shape[2]
    devices = lax.axis_size("tm")
    bus_blocks = bus_count // (devices * tile_width)
    total_hours = hour_rows * devices
    base_full = base_injection.astype(jnp.float32)
    inject = base_full
    level = soc_init
    line_dual = jnp.zeros((total_hours, line_count), jnp.float32)
    for iteration in range(ITERS):
        joined = jnp.concatenate([inject, level], axis=1)
        padded = padded_2(joined.astype(jnp.bfloat16), (("tm", 0),), 1).astype(joined.dtype)
        sent_rows = inject.astype(jnp.bfloat16)
        columns = lax.all_to_all(sent_rows, "tm", split_axis=1, concat_axis=0, tiled=True)
        columns = columns.reshape(total_hours, bus_blocks, tile_width)
        picked = columns[:, tile_block]
        partial_flow = jnp.einsum(
            "hgkb,gklb->hgl", picked, ptdf_tiles, preferred_element_type=jnp.float32
        )
        line_flows = lax.psum(partial_flow.reshape(total_hours, line_count), "tm")
        shifted = line_flows + line_dual
        clipped = jnp.clip(shifted, -limits, limits)
        line_dual = shifted - clipped
        dual_piece = line_dual.astype(jnp.bfloat16)
        piece_rows = dual_piece.shape[0]
        folded = dual_piece.reshape(piece_rows, groups, tile_width)
        contrib = jnp.einsum(
            "hgl,gklb->hgkb", folded, ptdf_tiles, preferred_element_type=jnp.float32
        )
        summed = (
            jnp.zeros((piece_rows, bus_blocks, tile_width), jnp.float32)
            .at[:, tile_block]
            .add(contrib)
        )
        price_cols = summed.reshape(piece_rows, bus_blocks * tile_width)
        bus_price = lax.all_to_all(price_cols, "tm", split_axis=0, concat_axis=1, tiled=True)
        prev_inj = padded[:-2, :bus_count]
        next_inj = padded[2:, :bus_count]
        prev_level = padded[:-2, bus_count:]
        store_price = bus_price[:, stor_bus]
        charge = level - prev_level
        updated = inject - step_size * (
            inject
            - base_full
            + penalty * bus_price
            + ramp_weight * (2.0 * inject - prev_inj - next_inj)
        )
        updated = updated.at[:, stor_bus].add(-step_size * charge)
        level = 0.5 * (level + prev_level) - stor_gain * store_price
        inject = updated
    own_dual = lax.dynamic_slice_in_dim(line_dual, lax.axis_index("tm") * hour_rows, hour_rows, 0)
    return (inject, own_dual, level)


def solution(mesh):
    in_specs = (
        P(("scen", "tm"), None),
        P(None, "tm", None, None),
        P(None, "tm"),
        P(),
        P(),
        P(),
        P(("scen", "tm"), None),
    )
    out_specs = (P(("scen", "tm"), None), P(("scen", "tm"), None), P(("scen", "tm"), None))
    return jax.shard_map(shards, mesh=mesh, in_specs=in_specs, out_specs=out_specs, check_vma=False)
```

profile of v0, /device:TPU:0, one launch (start us, length us, event | category | flops | bytes accessed | tf_op | source)
XLA Modules:
  0.0 460.8 jit_solution(3896762354028429285)
XLA Ops:
  10.3 7.4 %all-to-all-start = ((bf16[16,2,1152]{2,1,0:T(2,128)(2,1)}), bf16[16,2,1152]{2,1,0:T(2,128)(2,1)S(1)}, u32[]{:S(2)}, u32[]{:S(2)}) async-start(bf16[16,2,1152]{2,1,0:T(2,128)(2,1)} %reshape.246), calls=%async_computation | async-start | bytes 147456 | tf_op jit(solution)/shard_map/all_to_all | solution.py:45
  18.8 5.9 %all-to-all-done = bf16[16,2,1152]{2,1,0:T(2,128)(2,1)S(1)} async-done(((bf16[16,2,1152]{2,1,0:T(2,128)(2,1)}), bf16[16,2,1152]{2,1,0:T(2,128)(2,1)S(1)}, u32[]{:S(2)}, u32[]{:S(2)}) %all-to-all-start) | async-done | bytes 73760 | tf_op jit(solution)/shard_map/all_to_all | solution.py:45
  25.2 2.6 gather_fusion
  27.9 10.8 %convolution_bitcast_fusion.1 = f32[128,2,8,128]{3,2,1,0:T(8,128)S(1)} fusion(bf16[16,128,5,128]{3,0,2,1:T(8,128)(2,1)S(1)} %bitcast.86, bf16[128,5,128,128]{3,2,1,0:T(8,128)(2,1)} %param.8), kind=kOutput, calls=%fused_computation.9 | convolution fusion | flops 335544320 | bytes 24641536 | tf_op jit(solution)/shard_map/hgkb,gklb->hgl/dot_general | solution.py:48
  39.8 91.2 %all-reduce.3.cloned.1.call-done = f32[16,16384]{1,0:T(8,128)} async-done(((f32[16,16384]{1,0:T(8,128)}), f32[16,16384]{1,0:T(8,128)}) %all-reduce.3.cloned.1.call-update) | async-done | bytes 1048592 | tf_op jit(solution)/shard_map/psum | solution.py:51
  132.4 10.7 %fusion.4 = f32[128,16,5,128]{3,1,2,0:T(8,128)} fusion(bf16[128,5,128,128]{3,2,1,0:T(8,128)(2,1)} %param.8, bf16[16,128,128,1]{2,1,0,3:T(8,128)(2,1)S(1)} %bitcast.91), kind=kOutput, calls=%fused_computation.18 | convolution fusion | flops 335544320 | bytes 26738688 | tf_op jit(solution)/shard_map/hgl,gklb->hgkb/dot_general | solution.py:58
  143.2 50.9 %scatter_fusion = f32[16,18,128]{2,0,1:T(8,128)S(1)} fusion(f32[16,18,128]{2,0,1:T(8,128)S(1)} %broadcast.48.clone, s32[640]{0:T(1024)S(1)} %reshape.186, f32[640,16,128]{2,1,0:T(8,128)} %bitcast.84), kind=kCustom, calls=%fused_computation.4 | custom fusion | flops 1310720 | bytes 15731200 | tf_op jit(solution)/shard_map/scatter-add | solution.py:64
  195.0 3.8 all-to-all-start.1
  199.4 4.0 collective-permute-start.1
  203.5 4.0 all-to-all-done.1
  207.5 11.8 %gather_fusion.2 = f32[2048]{0:T(1024)S(1)} fusion(f32[36864]{0:T(1024)S(1)} %bitcast.79, s32[2048]{0:T(1024)S(1)} %get-tuple-element.10), kind=kCustom, calls=%fused_computation.2 | custom fusion | bytes 24576 | tf_op jit(solution)/shard_map/gather | solution.py:71
  220.9 11.5 %scatter_fusion.1 = f32[36864]{0:T(1024)S(1)} fusion(f32[36864]{0:T(1024)S(1)} %bitcast.76, s32[2048]{0:T(1024)S(1)} %get-tuple-element.11, f32[2048]{0:T(1024)S(1)} %bitcast.96), kind=kCustom, calls=%fused_computation.5 | custom fusion | flops 2048 | bytes 32768 | tf_op jit(solution)/shard_map/scatter-add | solution.py:79
  234.2 3.5 all-to-all-start.2
  238.0 6.7 %all-to-all-done.2 = bf16[16,2,1152]{2,1,0:T(2,128)(2,1)S(1)} async-done(((bf16[16,2,1152]{2,1,0:T(2,128)(2,1)}), bf16[16,2,1152]{2,1,0:T(2,128)(2,1)S(1)}, u32[]{:S(2)}, u32[]{:S(2)}) %all-to-all-start.2) | async-done | bytes 73760 | tf_op jit(solution)/shard_map/all_to_all | solution.py:45
  245.2 2.6 gather_fusion.1
  247.9 10.7 %convolution_bitcast_fusion = f32[128,2,8,128]{3,2,1,0:T(8,128)S(1)} fusion(bf16[16,128,5,128]{3,0,2,1:T(8,128)(2,1)S(1)} %bitcast.85, bf16[128,5,128,128]{3,2,1,0:T(8,128)(2,1)} %param.8), kind=kOutput, calls=%fused_computation.8 | convolution fusion | flops 335544320 | bytes 24641536 | tf_op jit(solution)/shard_map/hgkb,gklb->hgl/dot_general | solution.py:48
  260.0 4.4 collective-permute-start.3
  264.4 87.0 %all-reduce.5.cloned.1.call-done = f32[16,16384]{1,0:T(8,128)} async-done(((f32[16,16384]{1,0:T(8,128)}), f32[16,16384]{1,0:T(8,128)}) %all-reduce.5.cloned.1.call-update) | async-done | bytes 1048592 | tf_op jit(solution)/shard_map/psum | solution.py:51
  353.3 10.7 %fusion.2 = f32[128,16,5,128]{3,1,2,0:T(8,128)} fusion(bf16[128,5,128,128]{3,2,1,0:T(8,128)(2,1)} %param.8, bf16[16,128,128,1]{2,1,0,3:T(8,128)(2,1)S(1)} %bitcast.92), kind=kOutput, calls=%fused_computation.16 | convolution fusion | flops 335544320 | bytes 26738688 | tf_op jit(solution)/shard_map/hgl,gklb->hgkb/dot_general | solution.py:58
  364.1 50.9 %scatter_fusion.2 = f32[16,18,128]{2,0,1:T(8,128)S(1)} fusion(f32[16,18,128]{2,0,1:T(8,128)S(1)} %broadcast.48, s32[640]{0:T(1024)S(1)} %reshape.186, f32[640,16,128]{2,1,0:T(8,128)} %bitcast.83), kind=kCustom, calls=%fused_computation.6 | custom fusion | flops 1310720 | bytes 15731200 | tf_op jit(solution)/shard_map/scatter-add | solution.py:64
  415.9 3.8 all-to-all-start.3
  420.4 7.5 %all-to-all-done.3 = f32[16,1,2304]{2,1,0:T(1,128)S(1)} async-done(((f32[16,1,2304]{2,1,0:T(1,128)}), f32[16,1,2304]{2,1,0:T(1,128)S(1)}, u32[]{:S(2)}, u32[]{:S(2)}) %all-to-all-start.3) | async-done | bytes 147488 | tf_op jit(solution)/shard_map/all_to_all | solution.py:67
  427.8 11.8 %gather_fusion.3 = f32[2048]{0:T(1024)S(1)} fusion(f32[36864]{0:T(1024)S(1)} %bitcast.80, s32[2048]{0:T(1024)S(1)} %get-tuple-element.10), kind=kCustom, calls=%fused_computation.3 | custom fusion | bytes 24576 | tf_op jit(solution)/shard_map/gather | solution.py:71
  441.8 11.5 %scatter_fusion.3 = f32[36864]{0:T(1024)S(1)} fusion(f32[36864]{0:T(1024)S(1)} %bitcast.81, s32[2048]{0:T(1024)S(1)} %get-tuple-element.11, f32[2048]{0:T(1024)S(1)} %bitcast.95), kind=kCustom, calls=%fused_computation.7 | custom fusion | flops 2048 | bytes 32768 | tf_op jit(solution)/shard_map/scatter-add | solution.py:79
  (66 shorter events, 20.4 us)
Async XLA Ops:
  10.3 14.4 %all-to-all-start = ((bf16[16,2,1152]{2,1,0:T(2,128)(2,1)}), bf16[16,2,1152]{2,1,0:T(2,128)(2,1)S(1)}, u32[]{:S(2)}, u32[]{:S(2)}) async-start(bf16[16,2,1152]{2,1,0:T(2,128)(2,1)} %reshape.246), calls=%async_computation | async-start | bytes 147456 | tf_op jit(solution)/shard_map/all_to_all | solution.py:45
  17.7 113.2 %all-reduce.3.cloned.1.call-start = ((), (), s32[]{:S(2)}) async-start(), calls=%async_computation.4 | async-start | bytes 2097152 | tf_op jit(solution)/shard_map/psum | solution.py:51
  27.8 11.9 %copy-start.2 = (f32[16384]{0:T(1024)S(1)}, f32[16384]{0:T(1024)}, u32[]{:S(2)}) copy-start(f32[16384]{0:T(1024)} %param.10) | copy-start | bytes 196612
  27.8 11.9 %copy-start.3 = (f32[1,2048]{1,0:T(1,128)S(1)}, f32[1,2048]{1,0:T(1,128)}, u32[]{:S(2)}) copy-start(f32[1,2048]{1,0:T(1,128)} %param.13) | copy-start | bytes 24580
  143.1 55.6 %copy-start.1 = (bf16[1,36864]{1,0:T(2,128)(2,1)S(1)}, bf16[1,36864]{1,0:T(2,128)(2,1)}, u32[]{:S(2)}) copy-start(bf16[1,36864]{1,0:T(2,128)(2,1)} %param.7) | copy-start | bytes 221188
  143.2 60.3 %copy-start.5 = (s32[2048]{0:T(1024)S(1)}, s32[2048]{0:T(1024)}, u32[]{:S(2)}) copy-start(s32[2048]{0:T(1024)} %param.11) | copy-start | bytes 24580
  194.1 25.2 %copy-start.4 = (f32[2048]{0:T(1024)S(1)}, f32[2048]{0:T(1024)}, u32[]{:S(2)}) copy-start(f32[2048]{0:T(1024)} %param.12) | copy-start | bytes 24580
  195.0 12.5 %all-to-all-start.1 = ((f32[16,1,2304]{2,1,0:T(1,128)}), f32[16,1,2304]{2,1,0:T(1,128)S(1)}, u32[]{:S(2)}, u32[]{:S(2)}) async-start(f32[16,1,2304]{2,1,0:T(1,128)} %all_to_all.54), calls=%async_computation.1 | async-start | bytes 294912 | tf_op jit(solution)/shard_map/all_to_all | solution.py:67
  199.0 20.4 %collective-permute-start = (bf16[1,38912]{1,0:T(2,128)(2,1)S(1)}, bf16[1,38912]{1,0:T(2,128)(2,1)S(1)}, u32[]{:S(2)}, u32[]{:S(2)}) collective-permute-start(bf16[1,38912]{1,0:T(2,128)(2,1)S(1)} %pad_maximum_fusion), channel_id=1, source_target_pairs={{0,1},{1,2},{2,3},{3,4},{4,5},{5,6},{6,7},{7,8},{8,9},{9,10},{10,1... | collective-permute-start | bytes 233480 | tf_op jit(solution)/shard_map/ppermute | solution.py:20
  199.4 19.9 %collective-permute-start.1 = (bf16[1,38912]{1,0:T(2,128)(2,1)S(1)}, bf16[1,38912]{1,0:T(2,128)(2,1)S(1)}, u32[]{:S(2)}, u32[]{:S(2)}) collective-permute-start(bf16[1,38912]{1,0:T(2,128)(2,1)S(1)} %pad_maximum_fusion), channel_id=1, source_target_pairs={{1,0},{2,1},{3,2},{4,3},{5,4},{6,5},{7,6},{8,7},{9,8},{10,9},{11,1... | collective-permute-start | bytes 233480 | tf_op jit(solution)/shard_map/ppermute | solution.py:23
  234.2 10.5 %all-to-all-start.2 = ((bf16[16,2,1152]{2,1,0:T(2,128)(2,1)}), bf16[16,2,1152]{2,1,0:T(2,128)(2,1)S(1)}, u32[]{:S(2)}, u32[]{:S(2)}) async-start(bf16[16,2,1152]{2,1,0:T(2,128)(2,1)} %reshape.248), calls=%async_computation.2 | async-start | bytes 147456 | tf_op jit(solution)/shard_map/all_to_all | solution.py:45
  237.8 113.6 %all-reduce.5.cloned.1.call-start = ((), (), s32[]{:S(2)}) async-start(), calls=%async_computation.5 | async-start | bytes 2097152 | tf_op jit(solution)/shard_map/psum | solution.py:51
  259.9 179.7 %collective-permute-start.2 = (bf16[1,38912]{1,0:T(2,128)(2,1)S(1)}, bf16[1,38912]{1,0:T(2,128)(2,1)S(1)}, u32[]{:S(2)}, u32[]{:S(2)}) collective-permute-start(bf16[1,38912]{1,0:T(2,128)(2,1)S(1)} %pad_maximum_fusion.1), channel_id=1, source_target_pairs={{0,1},{1,2},{2,3},{3,4},{4,5},{5,6},{6,7},{7,8},{8,9},{9,10},{10,1... | collective-permute-start | bytes 233480 | tf_op jit(solution)/shard_map/ppermute | solution.py:20
  260.0 179.7 %collective-permute-start.3 = (bf16[1,38912]{1,0:T(2,128)(2,1)S(1)}, bf16[1,38912]{1,0:T(2,128)(2,1)S(1)}, u32[]{:S(2)}, u32[]{:S(2)}) collective-permute-start(bf16[1,38912]{1,0:T(2,128)(2,1)S(1)} %pad_maximum_fusion.1), channel_id=1, source_target_pairs={{1,0},{2,1},{3,2},{4,3},{5,4},{6,5},{7,6},{8,7},{9,8},{10,9},{11,1... | collective-permute-start | bytes 233480 | tf_op jit(solution)/shard_map/ppermute | solution.py:23
  415.9 12.0 %all-to-all-start.3 = ((f32[16,1,2304]{2,1,0:T(1,128)}), f32[16,1,2304]{2,1,0:T(1,128)S(1)}, u32[]{:S(2)}, u32[]{:S(2)}) async-start(f32[16,1,2304]{2,1,0:T(1,128)} %all_to_all.55), calls=%async_computation.3 | async-start | bytes 294912 | tf_op jit(solution)/shard_map/all_to_all | solution.py:67
  453.3 0.7 copy-start
Sparse Core Ops, SparseCore 0:
  39.8 91.0 all-reduce.2
  259.9 91.5 all-reduce.4
where the time goes:
time: 463 us; the launch traced here: 461 us
  waiting for transfers between devices  202 us (44%)
  other arithmetic  136 us (29%)
  matrix products  42.9 us (9%)
  local copies, waits for them, and re-layouts  37.4 us (8%)
  starting transfers between devices  27.7 us (6%)
  between operations  14.5 us (3%)
    psum x2, waiting for transfers between devices, shards(): line_flows = lax.psum(partial_flow.reshape(total_hours, line_count), 'tm')  178 us
    scatter-add x2, other arithmetic, shards(): summed = jnp.zeros((piece_rows, bus_blocks, tile_width), jnp.float32).at[...  102 us
    gather x2, local copies, waits for them, and re-layouts, shards(): store_price = bus_price[:, stor_bus]  23.5 us
    scatter-add x2, other arithmetic, shards(): updated = updated.at[:, stor_bus].add(-step_size * charge)  23.1 us
    dot_general x2, matrix products, shards(): jnp.einsum('hgkb,gklb->hgl', picked, ptdf_tiles, preferred_element_type=j...  21.5 us
    dot_general x2, matrix products, shards(): jnp.einsum('hgl,gklb->hgkb', folded, ptdf_tiles, preferred_element_type=j...  21.4 us
    all_to_all x2, waiting for transfers between devices, shards(): lax.all_to_all(sent_rows, 'tm', split_axis=1, concat_axis=0, tiled=True)  12.6 us
    all_to_all x2, waiting for transfers between devices, shards(): lax.all_to_all(price_cols, 'tm', split_axis=0, concat_axis=1, tiled=True)  11.5 us
  transfers between devices with their start and end apart: 10, of which 6 were waited for; matrix products, arithmetic and copies ran while one was open for 19% of the time, Pallas kernels for 0%

commit v1 on v0

v1 whole, which is shorter than its diff:
```python
import functools

import jax
import jax.numpy as jnp
from jax import lax
from jax.experimental import pallas as pl
from jax.experimental.pallas import tpu as pltpu
from jax.sharding import PartitionSpec as P

ITERS = 2

step_size = 0.5
penalty = 4.0
ramp_weight = 0.5

VM = pl.BlockSpec(memory_space=pltpu.VMEM)
MESH = pl.DeviceIdType.MESH


def peer(index):
    return {"tm": index}


def greet(others):
    barrier = pltpu.get_barrier_semaphore()
    for other in others:
        pl.semaphore_signal(barrier, inc=1, device_id=peer(other), device_id_type=MESH)
    pl.semaphore_wait(barrier, len(others))


def exchange_kernel(n, in_ref, out_ref, send_sem, recv_sem):
    me = lax.axis_index("tm")
    others = [lax.rem(me + k, n) for k in range(1, n)]
    greet(others)
    copies = []
    for k, other in enumerate(others):
        copy = pltpu.make_async_remote_copy(
            src_ref=in_ref.at[other],
            dst_ref=out_ref.at[me],
            send_sem=send_sem.at[k],
            recv_sem=recv_sem.at[k],
            device_id=peer(other),
            device_id_type=MESH,
        )
        copy.start()
        copies.append(copy)
    out_ref[me] = in_ref[me]
    for copy in copies:
        copy.wait()


def exchange(n, block, collective_id):
    return pl.pallas_call(
        functools.partial(exchange_kernel, n),
        out_shape=jax.ShapeDtypeStruct(block.shape, block.dtype),
        in_specs=[VM],
        out_specs=VM,
        scratch_shapes=[
            pltpu.SemaphoreType.DMA((n - 1,)),
            pltpu.SemaphoreType.DMA((n - 1,)),
        ],
        compiler_params=pltpu.CompilerParams(collective_id=collective_id, has_side_effects=True),
        name=f"exchange_{collective_id}",
    )(block)


def clip_kernel(
    n, hours, flow_ref, dual_ref, limits_ref, all_ref, own_ref,
    first_recv, first_sum, second_recv,
    pair_send, pair_recv, row_send, row_recv, out_send, out_recv, fwd_send, fwd_recv,
):
    half = n // 2
    me = lax.axis_index("tm")
    core = lax.rem(me, 2)
    spot = me // 2
    partner = me + 1 - 2 * core
    spots = [lax.rem(spot + k, half) for k in range(1, half)]
    greet([partner] + [s * 2 + core for s in spots])

    def remote(src, dst, send, recv, device):
        copy = pltpu.make_async_remote_copy(
            src_ref=src, dst_ref=dst, send_sem=send, recv_sem=recv,
            device_id=peer(device), device_id_type=MESH,
        )
        copy.start()
        return copy

    firsts = []
    for k, s in enumerate(spots + [spot]):
        firsts.append(remote(
            flow_ref.at[s, 1 - core], first_recv.at[k], pair_send.at[k], pair_recv.at[k], partner
        ))
    seconds = []
    for k, s in enumerate(spots):
        firsts[k].wait()
        first_sum[k] = (
            flow_ref[s, core].astype(jnp.float32) + first_recv[k].astype(jnp.float32)
        ).astype(jnp.bfloat16)
        seconds.append(remote(
            first_sum.at[k], second_recv.at[k], row_send.at[k], row_recv.at[k], s * 2 + core
        ))
    firsts[half - 1].wait()
    total = flow_ref[spot, core].astype(jnp.float32) + first_recv[half - 1].astype(jnp.float32)
    for k in range(half - 1):
        seconds[k].wait()
        total = total + second_recv[k].astype(jnp.float32)
    rows = total.shape[0]
    shifted = (total + dual_ref[...]).reshape(rows // hours, hours, total.shape[1])
    bound = limits_ref[...][:, None, :]
    clipped = jnp.minimum(jnp.maximum(shifted, -bound), bound)
    dual = (shifted - clipped).reshape(total.shape)
    own_ref[...] = dual
    all_ref[spot, core] = dual.astype(jnp.bfloat16)

    outs = []
    for k, s in enumerate(spots):
        outs.append(remote(
            all_ref.at[spot, core], all_ref.at[spot, core], out_send.at[k], out_recv.at[k], s * 2 + core
        ))
    forwards = [remote(
        all_ref.at[spot, core], all_ref.at[spot, core],
        fwd_send.at[half - 1], fwd_recv.at[half - 1], partner,
    )]
    for k in range(half - 1):
        outs[k].wait_recv()
        source = lax.rem(spot + half - k - 1, half)
        forwards.append(remote(
            all_ref.at[source, core], all_ref.at[source, core], fwd_send.at[k], fwd_recv.at[k], partner
        ))
    for copy in outs:
        copy.wait_send()
    for copy in forwards:
        copy.wait()


def clip_exchange(n, hours, flow, dual, limits, collective_id):
    half = n // 2
    chunk = dual.shape
    dma = pltpu.SemaphoreType.DMA
    return pl.pallas_call(
        functools.partial(clip_kernel, n, hours),
        out_shape=(
            jax.ShapeDtypeStruct((half, 2) + chunk, jnp.bfloat16),
            jax.ShapeDtypeStruct(chunk, jnp.float32),
        ),
        in_specs=[VM] * 3,
        out_specs=(VM, VM),
        scratch_shapes=[
            pltpu.VMEM((half,) + chunk, jnp.bfloat16),
            pltpu.VMEM((half - 1,) + chunk, jnp.bfloat16),
            pltpu.VMEM((half - 1,) + chunk, jnp.bfloat16),
            dma((half,)), dma((half,)),
            dma((half - 1,)), dma((half - 1,)),
            dma((half - 1,)), dma((half - 1,)),
            dma((half,)), dma((half,)),
        ],
        compiler_params=pltpu.CompilerParams(collective_id=collective_id, has_side_effects=True),
        name=f"clip_{collective_id}",
    )(flow.reshape((half, 2) + chunk), dual, limits)


def flow_kernel(block_ref, sent_ref, tiles_ref, out_ref):
    step = pl.program_id(0)
    count, depth = tiles_ref.shape[:2]
    for g in range(count):
        picked = jnp.concatenate(
            [sent_ref[block_ref[step * count + g, k]] for k in range(depth)], axis=1
        )
        wide = jnp.concatenate([tiles_ref[g, k] for k in range(depth)], axis=1)
        out_ref[g] = lax.dot_general(
            picked, wide, (((1,), (1,)), ((), ())), preferred_element_type=jnp.float32
        ).astype(out_ref.dtype)


def partial_flow(tile_block, sent, tiles, count):
    groups, depth, lines, width = tiles.shape
    blocks, hours = sent.shape[:2]
    return pl.pallas_call(
        flow_kernel,
        out_shape=jax.ShapeDtypeStruct((groups, hours, lines), jnp.bfloat16),
        grid_spec=pltpu.PrefetchScalarGridSpec(
            num_scalar_prefetch=1,
            grid=(groups // count,),
            in_specs=[
                pl.BlockSpec((blocks, hours, width), lambda i, b: (0, 0, 0)),
                pl.BlockSpec((count, depth, lines, width), lambda i, b: (i, 0, 0, 0)),
            ],
            out_specs=pl.BlockSpec((count, hours, lines), lambda i, b: (i, 0, 0)),
        ),
        name="flow",
    )(tile_block, sent, tiles)


def price_kernel(
    unit_chunk, block_ref, dual_ref, tiles_ref, base_ref, inj_ref, level_ref, gain_ref,
    unit_block_ref, unit_lane_ref, new_inj_ref, sent_ref, new_level_ref, *totals,
):
    step = pl.program_id(0)
    count, depth = tiles_ref.shape[:2]

    @pl.when(step == 0)
    def _():
        for total in totals:
            total[...] = jnp.zeros_like(total)

    for g in range(count):
        wide = jnp.concatenate([tiles_ref[g, k] for k in range(depth)], axis=1)
        part = jnp.dot(dual_ref[g], wide, preferred_element_type=jnp.float32)
        width = part.shape[1] // depth
        for k in range(depth):
            at = block_ref[step * count + g, k]
            totals[k][at] += part[:, k * width:(k + 1) * width]

    @pl.when(step == pl.num_programs(0) - 1)
    def _():
        price = totals[0][...]
        for total in totals[1:]:
            price = price + total[...]
        blocks, hours, width = price.shape
        units = level_ref.shape[1]
        flat = price.astype(jnp.bfloat16).reshape(blocks * hours, width)
        moved = jnp.zeros((blocks * hours, width), jnp.float32)
        for start in range(0, units, unit_chunk):
            span = pl.ds(start, unit_chunk)
            block = jnp.broadcast_to(unit_block_ref[:, span], (hours, unit_chunk))
            lane = unit_lane_ref[:, span]
            rows = lax.broadcasted_iota(jnp.int32, (width, unit_chunk), 0)
            chosen = jnp.where(rows == lane, 1.0, 0.0).astype(jnp.bfloat16)
            level = level_ref[:, span]
            before = pltpu.roll(level, 1, 0)
            charge = level - before
            spread = jnp.concatenate(
                [jnp.where(block == r, charge, 0.0).astype(jnp.bfloat16) for r in range(blocks)], axis=0
            )
            moved = moved + lax.dot_general(
                spread, chosen, (((1,), (1,)), ((), ())), preferred_element_type=jnp.float32
            )
            found = jnp.dot(flat, chosen, preferred_element_type=jnp.float32)
            store_price = jnp.zeros_like(level)
            for r in range(blocks):
                store_price = store_price + jnp.where(block == r, found[r * hours:(r + 1) * hours], 0.0)
            new_level_ref[:, span] = 0.5 * (level + before) - gain_ref[:, span] * store_price
        for r in range(blocks):
            inj = inj_ref[r].astype(jnp.float32)
            ramp = 2.0 * inj - pltpu.roll(inj, 1, 0) - pltpu.roll(inj, hours - 1, 0)
            updated = inj - step_size * (
                (inj - base_ref[r].astype(jnp.float32)) + penalty * price[r] + ramp_weight * ramp
            )
            updated = updated - step_size * moved[r * hours:(r + 1) * hours]
            new_inj_ref[r] = updated
            sent_ref[r] = updated.astype(jnp.bfloat16)


def price_update(tile_block, dual_all, tiles, base, inj, level, gain, unit_block, unit_lane, count):
    groups, depth, lines, width = tiles.shape
    blocks, hours = base.shape[:2]
    units = level.shape[1]
    chunk = 512 if units % 512 == 0 else units
    whole3 = pl.BlockSpec((blocks, hours, width), lambda i, b: (0, 0, 0))
    whole2 = pl.BlockSpec((hours, units), lambda i, b: (0, 0))
    line2 = pl.BlockSpec((1, units), lambda i, b: (0, 0))
    return pl.pallas_call(
        functools.partial(price_kernel, chunk),
        out_shape=(
            jax.ShapeDtypeStruct(base.shape, jnp.float32),
            jax.ShapeDtypeStruct(base.shape, jnp.bfloat16),
            jax.ShapeDtypeStruct(level.shape, jnp.float32),
        ),
        grid_spec=pltpu.PrefetchScalarGridSpec(
            num_scalar_prefetch=1,
            grid=(groups // count,),
            in_specs=[
                pl.BlockSpec((count, hours, lines), lambda i, b: (i, 0, 0)),
                pl.BlockSpec((count, depth, lines, width), lambda i, b: (i, 0, 0, 0)),
                whole3, whole3, whole2, line2, line2, line2,
            ],
            out_specs=(whole3, whole3, whole2),
            scratch_shapes=[pltpu.VMEM(base.shape, jnp.float32)] * depth,
        ),
        name="price",
    )(tile_block, dual_all, tiles, base, inj, level, gain, unit_block, unit_lane)


def shards(base_injection, ptdf_tiles, tile_block, limits, stor_bus, stor_gain, soc_init):
    n = lax.axis_size("tm")
    me = lax.axis_index("tm")
    hours = n * base_injection.shape[0]
    groups, _, lines, width = ptdf_tiles.shape
    units = soc_init.shape[1]
    unit_rows = units // width
    blocks = base_injection.shape[1] // (n * width)
    own_groups = groups // n
    count = 8

    opening = jnp.concatenate(
        [
            base_injection.reshape(n, blocks, width),
            jnp.broadcast_to(
                soc_init.astype(jnp.bfloat16).reshape(1, unit_rows, width), (n, unit_rows, width)
            ),
        ],
        axis=1,
    )
    opened = exchange(n, opening, 0)
    base = jnp.transpose(opened[:, :blocks], (1, 0, 2))
    level = opened[:, blocks:].reshape(hours, units).astype(jnp.float32)

    local_bus = stor_bus - me * (blocks * width)
    unit_block = jnp.floor_divide(local_bus, width).reshape(1, units)
    unit_lane = jnp.remainder(local_bus, width).reshape(1, units)
    gain = stor_gain.reshape(1, units)
    own_limits = lax.dynamic_slice_in_dim(limits.reshape(groups, lines), me * own_groups, own_groups, 0)

    inj, sent = base, base
    dual = jnp.zeros((own_groups * hours, lines), jnp.float32)
    for iteration in range(ITERS):
        flow = partial_flow(tile_block, sent, ptdf_tiles, count)
        dual_all, dual = clip_exchange(n, hours, flow, dual, own_limits, 1 + iteration)
        inj, sent, level = price_update(
            tile_block, dual_all.reshape(groups, hours, lines), ptdf_tiles, base, inj, level,
            gain, unit_block, unit_lane, count,
        )

    mine = (unit_block >= 0) & (unit_block < blocks)
    closing = jnp.concatenate(
        [
            jnp.transpose(inj, (1, 0, 2)),
            jnp.transpose(dual.reshape(own_groups, hours, lines), (1, 0, 2)),
            jnp.where(mine, level, 0.0).reshape(hours, unit_rows, width),
        ],
        axis=1,
    ).astype(jnp.bfloat16)
    closed = exchange(n, closing, 1 + ITERS).astype(jnp.float32)
    return (
        closed[:, :blocks].reshape(1, -1),
        closed[:, blocks:blocks + own_groups].reshape(1, -1),
        jnp.sum(closed[:, blocks + own_groups:], axis=0).reshape(1, -1),
    )


def solution(mesh):
    in_specs = (
        P(("scen", "tm"), None),
        P(None, "tm", None, None),
        P(None, "tm"),
        P(),
        P(),
        P(),
        P(("scen", "tm"), None),
    )
    out_specs = (P(("scen", "tm"), None), P(("scen", "tm"), None), P(("scen", "tm"), None))
    return jax.shard_map(shards, mesh=mesh, in_specs=in_specs, out_specs=out_specs, check_vma=False)
```

time: 463 us -> 162 us (0.35)
  waiting for transfers between devices: 202 us -> 0 us
  Pallas kernels: 0 us -> 139 us
  other arithmetic: 136 us -> 10.4 us
  matrix products: 42.9 us -> 0 us
  local copies, waits for them, and re-layouts: 37.4 us -> 9.01 us
  starting transfers between devices: 27.7 us -> 0 us
  between operations: 14.5 us -> 0.76 us
    psum x2 -> x0, waiting for transfers between devices: 178 us -> none  [shards(): line_flows = lax.psum(partial_flow.reshape(total_hours, line_count), 'tm')]
    pallas_call x0 -> x8, Pallas kernels: none -> 139 us  [the longest x2 44.5 us: clip_exchange(): pl.pallas_call(functools.partial(clip_kernel, n, hours), out_shape=(jax.S...]
    scatter-add x4 -> x0, other arithmetic: 125 us -> none  [the longest x2 102 us: shards(): summed = jnp.zeros((piece_rows, bus_blocks, tile_width), jnp.float32).at[...]
    dot_general x4 -> x0, matrix products: 42.9 us -> none  [the longest x2 21.5 us: shards(): jnp.einsum('hgkb,gklb->hgl', picked, ptdf_tiles, preferred_element_type=j...]
    gather x4 -> x0, local copies, waits for them, and re-layouts: 28.8 us -> none  [the longest x2 23.5 us: shards(): store_price = bus_price[:, stor_bus]]
    all_to_all x4 -> x0, waiting for transfers between devices: 24.1 us -> none  [the longest x2 12.6 us: shards(): lax.all_to_all(sent_rows, 'tm', split_axis=1, concat_axis=0, tiled=True)]
    all_to_all x4 -> x0, starting transfers between devices: 18.5 us -> none  [the longest x2 10.9 us: shards(): lax.all_to_all(sent_rows, 'tm', split_axis=1, concat_axis=0, tiled=True)]
    ppermute x4 -> x0, starting transfers between devices: 8.98 us -> none  [the longest x2 8.47 us: padded_2(): lax.ppermute(lax.slice_in_dim(block, 0, width, axis=dim), axis, backward)]
  transfers between devices with their start and end apart: 10 -> 0, of which waited for: 6 -> 0; matrix products, arithmetic and copies ran while one was open for 19% -> 0% of each run, Pallas kernels for 0% -> 0%
where the time goes in v1:
time: 162 us; the launch traced here: 159 us
  Pallas kernels  139 us (86%)
  other arithmetic  10.4 us (6%)
  local copies, waits for them, and re-layouts  9.01 us (6%)
    pallas_call x2, Pallas kernels, clip_exchange(): pl.pallas_call(functools.partial(clip_kernel, n, hours), out_shape=(jax.S...  44.5 us
    pallas_call x2, Pallas kernels, partial_flow(): pl.pallas_call(flow_kernel, out_shape=jax.ShapeDtypeStruct((groups, hours...  36.9 us
    pallas_call x2, Pallas kernels, price_update(): pl.pallas_call(functools.partial(price_kernel, chunk), out_shape=(jax.Sha...  35.9 us
    pallas_call x2, Pallas kernels, exchange(): pl.pallas_call(functools.partial(exchange_kernel, n), out_shape=jax.Shape...  22 us
    unnamed x8, local copies, waits for them, and re-layouts  3.6 us

profile of v1, /device:TPU:0, one launch (start us, length us, event | category | flops | bytes accessed | tf_op | source)
XLA Modules:
  0.0 159.4 jit_solution(8731694530738940863)
XLA Ops:
  0.6 0.8 copy-done
  2.1 0.7 convert_reduce_fusion
  2.8 1.3 add_select_fusion
  4.1 1.3 compare_and_fusion
  5.4 1.4 copy.27.block_ref
  6.8 1.3 reduce
  8.9 11.1 %exchange_0.1 = bf16[16,34,128]{2,1,0:T(8,128)(2,1)} custom-call(bf16[16,34,128]{2,1,0:T(8,128)(2,1)} %pad_maximum_fusion.1.in_ref), custom_call_target="tpu_custom_call" | custom-call | tf_op jit(solution)/shard_map/exchange_0/pallas_call | solution.py:53
  20.0 0.9 slice.15
  20.9 0.9 slice_convert_fusion
  22.5 0.7 copy.37
  23.2 18.4 %flow.2 = bf16[128,16,128]{2,1,0:T(8,128)(2,1)} custom-call(s32[128,5]{1,0:T(8,128)} %copy.27.block_ref, bf16[18,16,128]{2,1,0:T(8,128)(2,1)} %bitcast.31, bf16[128,5,128,128]{3,2,1,0:T(8,128)(2,1)} %tiles_ref.7), custom_call_target="tpu_custom_call" | custom-call | tf_op jit(solution)/shard_map/flow/pallas_call | solution.py:178
  42.3 22.4 %clip_1.1 = (bf16[8,2,128,128]{3,2,1,0:T(8,128)(2,1)}, f32[128,128]{1,0:T(8,128)}) custom-call(bf16[8,2,128,128]{3,2,1,0:T(8,128)(2,1)} %bitcast.30, f32[128,128]{1,0:T(8,128)} %broadcast_in_dim.24.dual_ref, f32[8,128]{1,0:T(8,128)} %constant_dynamic-slice_fusion.limits_ref), custom_call_target="tpu_custom_call" | custom-call | tf_op jit(solution)/shard_map/clip_1/pallas_call | solution.py:140
  64.6 17.9 %price.2 = (f32[18,16,128]{2,1,0:T(8,128)}, bf16[18,16,128]{2,1,0:T(8,128)(2,1)}, f32[16,2048]{1,0:T(8,128)}) custom-call(s32[128,5]{1,0:T(8,128)} %copy.27.block_ref, bf16[128,16,128]{2,1,0:T(8,128)(2,1)} %bitcast.37, bf16[128,5,128,128]{3,2,1,0:T(8,128)(2,1)} %tiles_ref.7, bf16[18,16,128]{2,1,0:T(8,128)(2,1)} %bitcast.32, bf16[18,16,128]{2,1,0:T(8,128)(2,1)} %bitcast.33, ...), custom_call_target="tpu_custom_call" | custom-call | tf_op jit(solution)/shard_map/price/pallas_call | solution.py:262
  82.5 18.4 %flow.3 = bf16[128,16,128]{2,1,0:T(8,128)(2,1)} custom-call(s32[128,5]{1,0:T(8,128)} %copy.27.block_ref, bf16[18,16,128]{2,1,0:T(8,128)(2,1)} %get-tuple-element.13.sent_ref, bf16[128,5,128,128]{3,2,1,0:T(8,128)(2,1)} %tiles_ref.7), custom_call_target="tpu_custom_call" | custom-call | tf_op jit(solution)/shard_map/flow/pallas_call | solution.py:178
  101.0 22.1 %clip_2.1 = (bf16[8,2,128,128]{3,2,1,0:T(8,128)(2,1)}, f32[128,128]{1,0:T(8,128)}) custom-call(bf16[8,2,128,128]{3,2,1,0:T(8,128)(2,1)} %bitcast.29, f32[128,128]{1,0:T(8,128)} %get-tuple-element.14.dual_ref, f32[8,128]{1,0:T(8,128)} %constant_dynamic-slice_fusion.limits_ref), custom_call_target="tpu_custom_call" | custom-call | tf_op jit(solution)/shard_map/clip_2/pallas_call | solution.py:140
  123.1 18.0 %price.3 = (f32[18,16,128]{2,1,0:T(8,128)}, bf16[18,16,128]{2,1,0:T(8,128)(2,1)}, f32[16,2048]{1,0:T(8,128)}) custom-call(s32[128,5]{1,0:T(8,128)} %copy.27.block_ref, bf16[128,16,128]{2,1,0:T(8,128)(2,1)} %bitcast.36, bf16[128,5,128,128]{3,2,1,0:T(8,128)(2,1)} %tiles_ref.7, bf16[18,16,128]{2,1,0:T(8,128)(2,1)} %bitcast.34, ...), custom_call_target="tpu_custom_call" | custom-call | tf_op jit(solution)/shard_map/price/pallas_call | solution.py:262
  141.1 0.9 convert.14
  142.1 0.9 fusion
  143.1 0.7 pad_maximum_fusion.in_ref
  143.8 10.9 %exchange_3.1 = bf16[16,42,128]{2,1,0:T(8,128)(2,1)} custom-call(bf16[16,42,128]{2,1,0:T(8,128)(2,1)} %pad_maximum_fusion.in_ref), custom_call_target="tpu_custom_call" | custom-call | tf_op jit(solution)/shard_map/exchange_3/pallas_call | solution.py:53
  154.6 1.5 slice.21
  156.1 0.9 slice.20
  157.0 0.8 reshape.70
  157.8 1.0 convert_element_type.15
  (14 shorter events, 3.3 us)
Async XLA Ops:
  0.6 0.8 copy-start
  123.1 19.0 %copy-start.1 = (f32[128,128]{1,0:T(8,128)S(1)}, f32[128,128]{1,0:T(8,128)}, u32[]{:S(2)}) copy-start(f32[128,128]{1,0:T(8,128)} %get-tuple-element.19) | copy-start | bytes 196612

commit v2 on v1

v2 whole, which is shorter than its diff:
```python
import functools

import jax
import jax.numpy as jnp
from jax import lax
from jax.experimental import pallas as pl
from jax.experimental.pallas import tpu as pltpu
from jax.sharding import PartitionSpec as P

ITERS = 2
STREAMS = 4

step_size = 0.5
penalty = 4.0
ramp_weight = 0.5

VM = pl.BlockSpec(memory_space=pltpu.VMEM)
MESH = pl.DeviceIdType.MESH


def peer(index):
    return {"tm": index}


def greet(others):
    barrier = pltpu.get_barrier_semaphore()
    for other in others:
        pl.semaphore_signal(barrier, inc=1, device_id=peer(other), device_id_type=MESH)
    pl.semaphore_wait(barrier, len(others))


def opening_kernel(n, base_ref, soc_ref, base_out, soc_out, send_sem, recv_sem):
    me = lax.axis_index("tm")
    width = base_out.shape[2]
    others = [lax.rem(me + k, n) for k in range(1, n)]
    greet(others)
    copies = []
    for k, other in enumerate(others):
        for part, (src, dst) in enumerate((
            (base_ref.at[:, pl.ds(pl.multiple_of(other * width, width), width)], base_out.at[me]),
            (soc_ref, soc_out.at[me]),
        )):
            copy = pltpu.make_async_remote_copy(
                src_ref=src, dst_ref=dst,
                send_sem=send_sem.at[part, k], recv_sem=recv_sem.at[part, k],
                device_id=peer(other), device_id_type=MESH,
            )
            copy.start()
            copies.append(copy)
    base_out[me] = base_ref[:, pl.ds(pl.multiple_of(me * width, width), width)]
    soc_out[me] = soc_ref[...]
    for copy in copies:
        copy.wait()


def opening(n, base, soc):
    return pl.pallas_call(
        functools.partial(opening_kernel, n),
        out_shape=(
            jax.ShapeDtypeStruct((n, 1, base.shape[1] // n), base.dtype),
            jax.ShapeDtypeStruct((n,) + soc.shape, soc.dtype),
        ),
        in_specs=[VM] * 2,
        out_specs=(VM, VM),
        scratch_shapes=[
            pltpu.SemaphoreType.DMA((2, n - 1)),
            pltpu.SemaphoreType.DMA((2, n - 1)),
        ],
        compiler_params=pltpu.CompilerParams(collective_id=0, has_side_effects=True),
        name="opening",
    )(base, soc)


def closing_kernel(
    n, inj_ref, dual_ref, level_ref, inj_out, dual_out, level_out,
    dual_rows, level_rows, level_recv, send_sem, recv_sem,
):
    me = lax.axis_index("tm")
    reach = inj_ref.shape[2]
    span = dual_rows.shape[2]
    width = dual_ref.shape[1]
    hours = dual_rows.shape[0]
    for h in range(hours):
        for g in range(span // width):
            dual_rows[h, :, g * width:(g + 1) * width] = dual_ref[g * hours + h:g * hours + h + 1, :]
    level_rows[...] = level_ref[...].astype(level_rows.dtype)
    others = [lax.rem(me + k, n) for k in range(1, n)]
    greet(others)
    inj_here = inj_out.at[:, pl.ds(pl.multiple_of(me * reach, reach), reach)]
    dual_here = dual_out.at[:, pl.ds(pl.multiple_of(me * span, span), span)]
    copies = []
    for k, other in enumerate(others):
        for part, (src, dst) in enumerate((
            (inj_ref.at[other], inj_here),
            (dual_rows.at[other], dual_here),
            (level_rows.at[other], level_recv.at[k]),
        )):
            copy = pltpu.make_async_remote_copy(
                src_ref=src, dst_ref=dst,
                send_sem=send_sem.at[part, k], recv_sem=recv_sem.at[part, k],
                device_id=peer(other), device_id_type=MESH,
            )
            copy.start()
            copies.append(copy)
    inj_here[...] = inj_ref[me]
    dual_here[...] = dual_rows[me]
    for copy in copies:
        copy.wait()
    level = level_ref[me]
    for k in range(n - 1):
        level = level + level_recv[k].astype(jnp.float32)
    for q in range(level.shape[0]):
        level_out[:, q * width:(q + 1) * width] = level[q:q + 1]


def closing(n, inj, dual, level, collective_id):
    hours, _, reach = inj.shape
    rows, width = dual.shape
    span = rows // hours * width
    return pl.pallas_call(
        functools.partial(closing_kernel, n),
        out_shape=(
            jax.ShapeDtypeStruct((1, n * reach), jnp.float32),
            jax.ShapeDtypeStruct((1, n * span), jnp.float32),
            jax.ShapeDtypeStruct((1, level.shape[1] * level.shape[2]), jnp.float32),
        ),
        in_specs=[VM] * 3,
        out_specs=(VM, VM, VM),
        scratch_shapes=[
            pltpu.VMEM((hours, 1, span), jnp.float32),
            pltpu.VMEM(level.shape, jnp.bfloat16),
            pltpu.VMEM((n - 1,) + level.shape[1:], jnp.bfloat16),
            pltpu.SemaphoreType.DMA((3, n - 1)),
            pltpu.SemaphoreType.DMA((3, n - 1)),
        ],
        compiler_params=pltpu.CompilerParams(collective_id=collective_id, has_side_effects=True),
        name="closing",
    )(inj, dual, level)


def clip_kernel(
    n, hours, flow_ref, dual_ref, limits_ref, all_ref, own_ref,
    first_recv, first_sum, second_recv,
    pair_send, pair_recv, row_send, row_recv, out_send, out_recv, fwd_send, fwd_recv,
):
    half = n // 2
    me = lax.axis_index("tm")
    core = lax.rem(me, 2)
    spot = me // 2
    partner = me + 1 - 2 * core
    spots = [lax.rem(spot + k, half) for k in range(1, half)]
    greet([partner] + [s * 2 + core for s in spots])

    def remote(src, dst, send, recv, device):
        copy = pltpu.make_async_remote_copy(
            src_ref=src, dst_ref=dst, send_sem=send, recv_sem=recv,
            device_id=peer(device), device_id_type=MESH,
        )
        copy.start()
        return copy

    firsts = []
    for k, s in enumerate(spots + [spot]):
        firsts.append(remote(
            flow_ref.at[s, 1 - core], first_recv.at[k], pair_send.at[k], pair_recv.at[k], partner
        ))
    seconds = []
    for k, s in enumerate(spots):
        firsts[k].wait()
        first_sum[k] = (
            flow_ref[s, core] + first_recv[k]
        ).astype(jnp.bfloat16)
        seconds.append(remote(
            first_sum.at[k], second_recv.at[k], row_send.at[k], row_recv.at[k], s * 2 + core
        ))
    firsts[half - 1].wait()
    total = flow_ref[spot, core] + first_recv[half - 1]
    for k in range(half - 1):
        seconds[k].wait()
        total = total + second_recv[k].astype(jnp.float32)
    rows = total.shape[0]
    shifted = (total + dual_ref[...]).reshape(rows // hours, hours, total.shape[1])
    bound = limits_ref[...][:, None, :]
    clipped = jnp.minimum(jnp.maximum(shifted, -bound), bound)
    dual = (shifted - clipped).reshape(total.shape)
    own_ref[...] = dual
    all_ref[spot, core] = dual.astype(jnp.bfloat16)

    outs = []
    for k, s in enumerate(spots):
        outs.append(remote(
            all_ref.at[spot, core], all_ref.at[spot, core], out_send.at[k], out_recv.at[k], s * 2 + core
        ))
    forwards = [remote(
        all_ref.at[spot, core], all_ref.at[spot, core],
        fwd_send.at[half - 1], fwd_recv.at[half - 1], partner,
    )]
    for k in range(half - 1):
        outs[k].wait_recv()
        source = lax.rem(spot + half - k - 1, half)
        forwards.append(remote(
            all_ref.at[source, core], all_ref.at[source, core], fwd_send.at[k], fwd_recv.at[k], partner
        ))
    for copy in outs:
        copy.wait_send()
    for copy in forwards:
        copy.wait()


def clip_exchange(n, hours, flow, dual, limits, collective_id):
    half = n // 2
    chunk = dual.shape
    dma = pltpu.SemaphoreType.DMA
    return pl.pallas_call(
        functools.partial(clip_kernel, n, hours),
        out_shape=(
            jax.ShapeDtypeStruct((half, 2) + chunk, jnp.bfloat16),
            jax.ShapeDtypeStruct(chunk, jnp.float32),
        ),
        in_specs=[VM] * 3,
        out_specs=(VM, VM),
        scratch_shapes=[
            pltpu.VMEM((half,) + chunk, jnp.float32),
            pltpu.VMEM((half - 1,) + chunk, jnp.bfloat16),
            pltpu.VMEM((half - 1,) + chunk, jnp.bfloat16),
            dma((half,)), dma((half,)),
            dma((half - 1,)), dma((half - 1,)),
            dma((half - 1,)), dma((half - 1,)),
            dma((half,)), dma((half,)),
        ],
        compiler_params=pltpu.CompilerParams(collective_id=collective_id, has_side_effects=True),
        name=f"clip_{collective_id}",
    )(flow.reshape((half, 2) + chunk), dual, limits)


def flow_kernel(block_ref, sent_ref, *refs):
    step = pl.program_id(0)
    tile_refs, out_ref = refs[:-1], refs[-1]
    each, depth = tile_refs[0].shape[:2]
    count = each * len(tile_refs)
    for g in range(count):
        picked = jnp.concatenate(
            [sent_ref[block_ref[step * count + g, k]] for k in range(depth)], axis=1
        )
        wide = jnp.concatenate([tile_refs[g // each][g % each, k] for k in range(depth)], axis=1)
        out_ref[g] = lax.dot_general(
            picked, wide, (((1,), (1,)), ((), ())), preferred_element_type=jnp.float32
        ).astype(out_ref.dtype)


def tile_specs(tiles, count):
    shape = (count // STREAMS,) + tiles.shape[1:]
    return [
        pl.BlockSpec(shape, lambda i, b, part=part: (i * STREAMS + part, 0, 0, 0))
        for part in range(STREAMS)
    ]


def partial_flow(tile_block, sent, tiles, count):
    groups, depth, lines, width = tiles.shape
    blocks, hours = sent.shape[:2]
    return pl.pallas_call(
        flow_kernel,
        out_shape=jax.ShapeDtypeStruct((groups, hours, lines), jnp.float32),
        grid_spec=pltpu.PrefetchScalarGridSpec(
            num_scalar_prefetch=1,
            grid=(groups // count,),
            in_specs=[
                pl.BlockSpec((blocks, hours, width), lambda i, b: (0, 0, 0)),
                *tile_specs(tiles, count),
            ],
            out_specs=pl.BlockSpec((count, hours, lines), lambda i, b: (i, 0, 0)),
        ),
        name="flow",
    )(tile_block, sent, *([tiles] * STREAMS))


def price_kernel(
    unit_chunk, last, depth, block_ref, dual_ref, *refs
):
    step = pl.program_id(0)
    tile_refs, refs = refs[:STREAMS], refs[STREAMS:]
    base_ref, inj_ref, level_ref, gain_ref, unit_ref, new_inj_ref, second_ref, new_level_ref = refs[:-depth]
    totals = refs[-depth:]
    each = tile_refs[0].shape[0]
    count = each * STREAMS

    @pl.when(step == 0)
    def _():
        for total in totals:
            total[...] = jnp.zeros_like(total)

    for g in range(count):
        wide = jnp.concatenate([tile_refs[g // each][g % each, k] for k in range(depth)], axis=1)
        part = jnp.dot(dual_ref[g], wide, preferred_element_type=jnp.float32)
        width = part.shape[1] // depth
        for k in range(depth):
            at = block_ref[step * count + g, k]
            totals[k][at] += part[:, k * width:(k + 1) * width]

    @pl.when(step == pl.num_programs(0) - 1)
    def _():
        price = totals[0][...]
        for total in totals[1:]:
            price = price + total[...]
        blocks, hours, width = price.shape
        units = level_ref.shape[1]
        flat = price.astype(jnp.bfloat16).reshape(blocks * hours, width)
        moved = jnp.zeros((blocks * hours, width), jnp.float32)
        for start in range(0, units, unit_chunk):
            span = pl.ds(start, unit_chunk)
            bus = unit_ref[:, span]
            first = lax.axis_index("tm") * blocks
            block = jnp.broadcast_to(lax.div(bus, width) - first, (hours, unit_chunk))
            lane = lax.rem(bus, width)
            rows = lax.broadcasted_iota(jnp.int32, (width, unit_chunk), 0)
            chosen = jnp.where(rows == lane, 1.0, 0.0).astype(jnp.bfloat16)
            level = level_ref[:, span]
            before = pltpu.roll(level, 1, 0)
            charge = level - before
            spread = jnp.concatenate(
                [jnp.where(block == r, charge, 0.0).astype(jnp.bfloat16) for r in range(blocks)], axis=0
            )
            moved = moved + lax.dot_general(
                spread, chosen, (((1,), (1,)), ((), ())), preferred_element_type=jnp.float32
            )
            found = jnp.dot(flat, chosen, preferred_element_type=jnp.float32)
            store_price = jnp.zeros_like(level)
            for r in range(blocks):
                store_price = store_price + jnp.where(block == r, found[r * hours:(r + 1) * hours], 0.0)
            new_level = 0.5 * (level + before) - gain_ref[:, span] * store_price
            if last:
                new_level = jnp.where((block >= 0) & (block < blocks), new_level, 0.0)
                for q in range(unit_chunk // width):
                    new_level_ref[:, start // width + q, :] = new_level[:, q * width:(q + 1) * width]
            else:
                new_level_ref[:, span] = new_level
        for r in range(blocks):
            inj = inj_ref[r].astype(jnp.float32)
            ramp = 2.0 * inj - pltpu.roll(inj, 1, 0) - pltpu.roll(inj, hours - 1, 0)
            updated = inj - step_size * (
                (inj - base_ref[r].astype(jnp.float32)) + penalty * price[r] + ramp_weight * ramp
            )
            updated = updated - step_size * moved[r * hours:(r + 1) * hours]
            if last:
                for h in range(hours):
                    new_inj_ref[h, :, r * width:(r + 1) * width] = updated[h:h + 1]
            else:
                new_inj_ref[r] = updated
                second_ref[r] = updated.astype(jnp.bfloat16)
        if last:
            second_ref[...] = jnp.zeros_like(second_ref)


def price_update(last, tile_block, dual_all, tiles, base, inj, level, gain, unit_bus, count):
    groups, depth, lines, width = tiles.shape
    blocks, hours = base.shape[:2]
    units = level.shape[1]
    chunk = 512 if units % 512 == 0 else units
    whole3 = pl.BlockSpec((blocks, hours, width), lambda i, b: (0, 0, 0))
    whole2 = pl.BlockSpec((hours, units), lambda i, b: (0, 0))
    line2 = pl.BlockSpec((1, units), lambda i, b: (0, 0))
    if last:
        outs = (
            ((hours, 1, blocks * width), jnp.float32),
            ((8, 128), jnp.float32),
            ((hours, units // width, width), jnp.float32),
        )
    else:
        outs = ((base.shape, jnp.float32), (base.shape, jnp.bfloat16), (level.shape, jnp.float32))
    return pl.pallas_call(
        functools.partial(price_kernel, chunk, last, depth),
        out_shape=tuple(jax.ShapeDtypeStruct(*out) for out in outs),
        grid_spec=pltpu.PrefetchScalarGridSpec(
            num_scalar_prefetch=1,
            grid=(groups // count,),
            in_specs=[
                pl.BlockSpec((count, hours, lines), lambda i, b: (i, 0, 0)),
                *tile_specs(tiles, count),
                whole3, whole3, whole2, line2, line2,
            ],
            out_specs=tuple(
                pl.BlockSpec(shape, lambda i, b, rank=len(shape): (0,) * rank) for shape, _ in outs
            ),
            scratch_shapes=[pltpu.VMEM(base.shape, jnp.float32)] * depth,
        ),
        name="price",
    )(tile_block, dual_all, *([tiles] * STREAMS), base, inj, level, gain, unit_bus)


def shards(base_injection, ptdf_tiles, tile_block, limits, stor_bus, stor_gain, soc_init):
    n = lax.axis_size("tm")
    me = lax.axis_index("tm")
    hours = n * base_injection.shape[0]
    groups, _, lines, width = ptdf_tiles.shape
    units = soc_init.shape[1]
    blocks = base_injection.shape[1] // (n * width)
    own_groups = groups // n
    count = 32

    base, level = opening(n, base_injection, soc_init)
    base = jnp.transpose(base.reshape(hours, blocks, width), (1, 0, 2))
    level = level.reshape(hours, units)

    unit_bus = stor_bus.reshape(1, units)
    gain = stor_gain.reshape(1, units)
    own_limits = lax.dynamic_slice_in_dim(limits.reshape(groups, lines), me * own_groups, own_groups, 0)

    inj, sent = base, base
    dual = jnp.zeros((own_groups * hours, lines), jnp.float32)
    for iteration in range(ITERS):
        flow = partial_flow(tile_block, sent, ptdf_tiles, count)
        dual_all, dual = clip_exchange(n, hours, flow, dual, own_limits, 1 + iteration)
        inj, sent, level = price_update(
            iteration == ITERS - 1, tile_block, dual_all.reshape(groups, hours, lines), ptdf_tiles,
            base, inj, level, gain, unit_bus, count,
        )
    return closing(n, inj, dual, level, 1 + ITERS)


def solution(mesh):
    in_specs = (
        P(("scen", "tm"), None),
        P(None, "tm", None, None),
        P(None, "tm"),
        P(),
        P(),
        P(),
        P(("scen", "tm"), None),
    )
    out_specs = (P(("scen", "tm"), None), P(("scen", "tm"), None), P(("scen", "tm"), None))
    return jax.shard_map(shards, mesh=mesh, in_specs=in_specs, out_specs=out_specs, check_vma=False)
```

time: 162 us -> 137 us (0.85); the launches traced: 159 us -> 137 us
  Pallas kernels: 139 us -> 125 us
  other arithmetic: 10.4 us -> 1.31 us
    pallas_call x2, Pallas kernels: 36.9 us -> 26.6 us  [partial_flow(): pl.pallas_call(flow_kernel, out_shape=jax.ShapeDtypeStruct((groups, hours...]
    pallas_call x4, Pallas kernels: 57.9 us -> 52.3 us  [the longest x2 26.4 us: price_update(): pl.pallas_call(functools.partial(price_kernel, chunk, last, depth), out_s...]
    unnamed x8 -> x7, local copies, waits for them, and re-layouts: 3.6 us -> 8.19 us
    slice x3 -> x0, local copies, waits for them, and re-layouts: 3.3 us -> none  [the longest x1 1.49 us: shards(): closed[:, blocks:blocks + own_groups].reshape(1, -1)]
    convert_element_type x3 -> x0, other arithmetic: 2.59 us -> none  [the longest x1 0.95 us: shards(): closed = exchange(n, closing, 1 + ITERS).astype(jnp.float32)]
    unnamed x2 -> x0, other arithmetic: 2.24 us -> none
where the time goes in v2:
time: 137 us
  Pallas kernels  125 us (91%)
  local copies, waits for them, and re-layouts  10.1 us (7%)
    pallas_call x2, Pallas kernels, clip_exchange(): pl.pallas_call(functools.partial(clip_kernel, n, hours), out_shape=(jax.S...  45.7 us
    pallas_call x2, Pallas kernels, partial_flow(): pl.pallas_call(flow_kernel, out_shape=jax.ShapeDtypeStruct((groups, hours...  26.6 us
    pallas_call x2, Pallas kernels, price_update(): pl.pallas_call(functools.partial(price_kernel, chunk, last, depth), out_s...  26.4 us
    pallas_call x1, Pallas kernels, opening(): pl.pallas_call(functools.partial(opening_kernel, n), out_shape=(jax.Shape...  13.2 us
    pallas_call x1, Pallas kernels, closing(): pl.pallas_call(functools.partial(closing_kernel, n), out_shape=(jax.Shape...  12.7 us
    unnamed x7, local copies, waits for them, and re-layouts  8.19 us

profile of v2, /device:TPU:0, one launch (start us, length us, event | category | flops | bytes accessed | tf_op | source)
XLA Modules:
  0.0 136.7 jit_solution(2189291647634926326)
XLA Ops:
  0.6 0.0 copy-start
  0.6 0.8 copy-done
  1.5 0.6 constant_dynamic-slice_fusion.limits_ref
  2.1 1.4 %copy.18.block_ref = s32[128,5]{1,0:T(8,128)} copy(s32[128,5]{0,1:T(8,128)} %param.9) | data formatting | bytes 5120 | tf_op args[2]
  3.5 13.2 %opening.1 = (bf16[16,1,2304]{2,1,0:T(2,128)(2,1)}, f32[16,1,2048]{2,1,0:T(1,128)}) custom-call(bf16[1,36864]{1,0:T(2,128)(2,1)} %base_ref.1, f32[1,2048]{1,0:T(1,128)} %soc_ref.1), custom_call_target="tpu_custom_call" | custom-call | tf_op jit(solution)/shard_map/opening/pallas_call | solution.py:57
  16.7 1.3 reduce
  18.0 0.6 bitcast_bitcast_fusion.sent_ref.refs_4_.refs_5_
  18.7 1.6 %copy.23 = f32[16,1,2048]{2,0,1:T(8,128)} copy(f32[16,1,2048]{2,1,0:T(1,128)} %get-tuple-element.16) | data formatting | bytes 262144
  20.3 13.3 %flow.2 = f32[128,16,128]{2,1,0:T(8,128)} custom-call(s32[128,5]{1,0:T(8,128)} %copy.18.block_ref, bf16[18,16,128]{2,1,0:T(8,128)(2,1)} %bitcast_bitcast_fusion.sent_ref.refs_4_.refs_5_, bf16[128,5,128,128]{3,2,1,0:T(8,128)(2,1)} %refs_3_.7, bf16[128,5,128,128]{3,2,1,0:T(8,128)(2,1)} %refs_3_.7, bf16[128,5,128,128]{3,2,1,0:T(8,128)(2,1)} %refs_3_.7, ...), custom_call_target="tpu_custom_call" | custom-call | tf_op jit(solution)/shard_map/flow/pallas_call | solution.py:262
  33.6 0.6 broadcast_in_dim.3.dual_ref
  34.2 23.3 %clip_1.1 = (bf16[8,2,128,128]{3,2,1,0:T(8,128)(2,1)}, f32[128,128]{1,0:T(8,128)}) custom-call(f32[8,2,128,128]{3,2,1,0:T(8,128)} %bitcast.19, f32[128,128]{1,0:T(8,128)} %broadcast_in_dim.3.dual_ref, f32[8,128]{1,0:T(8,128)} %constant_dynamic-slice_fusion.limits_ref), custom_call_target="tpu_custom_call" | custom-call | tf_op jit(solution)/shard_map/clip_1/pallas_call | solution.py:214
  57.5 13.4 %price.2 = (f32[18,16,128]{2,1,0:T(8,128)}, bf16[18,16,128]{2,1,0:T(8,128)(2,1)}, f32[16,2048]{1,0:T(8,128)}) custom-call(s32[128,5]{1,0:T(8,128)} %copy.18.block_ref, bf16[128,16,128]{2,1,0:T(8,128)(2,1)} %bitcast.21, bf16[128,5,128,128]{3,2,1,0:T(8,128)(2,1)} %refs_3_.7, bf16[128,5,128,128]{3,2,1,0:T(8,128)(2,1)} %refs_3_.7, ...), custom_call_target="tpu_custom_call" | custom-call | tf_op jit(solution)/shard_map/price/pallas_call | solution.py:371
  70.9 13.3 %flow.3 = f32[128,16,128]{2,1,0:T(8,128)} custom-call(s32[128,5]{1,0:T(8,128)} %copy.18.block_ref, bf16[18,16,128]{2,1,0:T(8,128)(2,1)} %get-tuple-element.17.sent_ref, bf16[128,5,128,128]{3,2,1,0:T(8,128)(2,1)} %refs_3_.7, bf16[128,5,128,128]{3,2,1,0:T(8,128)(2,1)} %refs_3_.7, bf16[128,5,128,128]{3,2,1,0:T(8,128)(2,1)} %refs_3_.7, ...), custom_call_target="tpu_custom_call" | custom-call | tf_op jit(solution)/shard_map/flow/pallas_call | solution.py:262
  84.2 22.4 %clip_2.1 = (bf16[8,2,128,128]{3,2,1,0:T(8,128)(2,1)}, f32[128,128]{1,0:T(8,128)}) custom-call(f32[8,2,128,128]{3,2,1,0:T(8,128)} %bitcast.18, f32[128,128]{1,0:T(8,128)} %get-tuple-element.18.dual_ref, f32[8,128]{1,0:T(8,128)} %constant_dynamic-slice_fusion.limits_ref), custom_call_target="tpu_custom_call" | custom-call | tf_op jit(solution)/shard_map/clip_2/pallas_call | solution.py:214
  106.7 13.0 %price.3 = (f32[16,1,2304]{2,1,0:T(1,128)}, f32[8,128]{1,0:T(8,128)}, f32[16,16,128]{2,1,0:T(8,128)}) custom-call(s32[128,5]{1,0:T(8,128)} %copy.18.block_ref, bf16[128,16,128]{2,1,0:T(8,128)(2,1)} %bitcast.20, bf16[128,5,128,128]{3,2,1,0:T(8,128)(2,1)} %refs_3_.7, bf16[128,5,128,128]{3,2,1,0:T(8,128)(2,1)} %refs_3_.7, bf16[128,5,128,128]{3,2,1,0:T(8,128)(2,1)} %refs_3_.7, ...), custom_call_target="tpu_custom_call" | custom-call | tf_op jit(solution)/shard_map/price/pallas_call | solution.py:371
  119.6 12.7 %closing.1 = (f32[1,36864]{1,0:T(1,128)}, f32[1,16384]{1,0:T(1,128)}, f32[1,2048]{1,0:T(1,128)}) custom-call(f32[16,1,2304]{2,1,0:T(1,128)} %get-tuple-element.22.inj_ref, f32[128,128]{1,0:T(8,128)} %get-tuple-element.23.dual_ref, f32[16,16,128]{2,1,0:T(8,128)} %get-tuple-element.24.level_ref), custom_call_target="tpu_custom_call" | custom-call | tf_op jit(solution)/shard_map/closing/pallas_call | solution.py:120
  132.3 1.6 %copy.27 = f32[1,36864]{1,0:T(1,128)} copy(f32[1,36864]{1,0:T(1,128)} %get-tuple-element.28) | data formatting | bytes 294912
  133.9 1.5 %copy.28 = f32[1,16384]{1,0:T(1,128)} copy(f32[1,16384]{1,0:T(1,128)} %get-tuple-element.29) | data formatting | bytes 131072
  135.4 1.3 copy.29
Async XLA Ops:
  0.6 0.8 copy-start

commit v3 on v2

--- a/solution.py
+++ b/solution.py
@@ -138,45 +138,87 @@
     )(inj, dual, level)
 
 
-def clip_kernel(
-    n, hours, flow_ref, dual_ref, limits_ref, all_ref, own_ref,
-    first_recv, first_sum, second_recv,
-    pair_send, pair_recv, row_send, row_recv, out_send, out_recv, fwd_send, fwd_recv,
+def flow_clip_kernel(
+    n, hours, block_ref, sent_ref, dual_ref, limits_ref, tiles_ref, all_ref, own_ref,
+    held, theirs, mine, first_recv, first_sum, second_recv,
+    tile_sem, pair_send, pair_recv, row_send, row_recv,
+    far_send, far_recv, mid_send, mid_recv, near_send, near_recv,
 ):
-    half = n // 2
+    half, quarter = n // 2, n // 4
     me = lax.axis_index("tm")
     core = lax.rem(me, 2)
     spot = me // 2
     partner = me + 1 - 2 * core
+    slots, own_groups, depth = held.shape[:3]
     spots = [lax.rem(spot + k, half) for k in range(1, half)]
-    greet([partner] + [s * 2 + core for s in spots])
 
     def remote(src, dst, send, recv, device):
-        copy = pltpu.make_async_remote_copy(
+        return pltpu.make_async_remote_copy(
             src_ref=src, dst_ref=dst, send_sem=send, recv_sem=recv,
             device_id=peer(device), device_id_type=MESH,
         )
-        copy.start()
-        return copy
-
-    firsts = []
-    for k, s in enumerate(spots + [spot]):
-        firsts.append(remote(
-            flow_ref.at[s, 1 - core], first_recv.at[k], pair_send.at[k], pair_recv.at[k], partner
-        ))
-    seconds = []
-    for k, s in enumerate(spots):
-        firsts[k].wait()
-        first_sum[k] = (
-            flow_ref[s, core] + first_recv[k]
-        ).astype(jnp.bfloat16)
-        seconds.append(remote(
-            first_sum.at[k], second_recv.at[k], row_send.at[k], row_recv.at[k], s * 2 + core
-        ))
-    firsts[half - 1].wait()
-    total = flow_ref[spot, core] + first_recv[half - 1]
+
+    def owner(k, other):
+        return lax.rem(spot + k + 1, half) * 2 + (1 - core if other else core)
+
+    def fetch(k, other, slot):
+        return pltpu.make_async_copy(
+            tiles_ref.at[pl.ds(owner(k, other) * own_groups, own_groups)], held.at[slot], tile_sem.at[slot]
+        )
+
+    def product(k, other, slot, out):
+        first = owner(k, other) * own_groups
+        for g in range(own_groups):
+            picked = jnp.concatenate([sent_ref[block_ref[first + g, t]] for t in range(depth)], axis=1)
+            wide = jnp.concatenate([held[slot, g, t] for t in range(depth)], axis=1)
+            out[k, g * hours:(g + 1) * hours] = lax.dot_general(
+                picked, wide, (((1,), (1,)), ((), ())), preferred_element_type=jnp.float32
+            )
+
+    def pair(k):
+        return remote(theirs.at[k], first_recv.at[k], pair_send.at[k], pair_recv.at[k], partner)
+
+    def row(k):
+        return remote(
+            first_sum.at[k], second_recv.at[k], row_send.at[k], row_recv.at[k],
+            lax.rem(spot + k + 1, half) * 2 + core,
+        )
+
+    ahead = slots // 2
+    for k in range(ahead):
+        fetch(k, True, 2 * k).start()
+        fetch(k, False, 2 * k + 1).start()
+    greet([partner] + [s * 2 + core for s in spots])
+
+    def pass_on(k):
+        pair(k).wait_recv()
+        first_sum[k] = (mine[k] + first_recv[k]).astype(jnp.bfloat16)
+        row(k).start()
+
+    def step(k, carry):
+        slot = lax.rem(k, ahead) * 2
+        for other, out in ((True, theirs), (False, mine)):
+            place = slot if other else slot + 1
+            fetch(k, other, place).wait()
+            product(k, other, place, out)
+            if other:
+                pair(k).start()
+
+            @pl.when(k + ahead < half)
+            def _():
+                fetch(k + ahead, other, place).start()
+
+        @pl.when(k >= 1)
+        def _():
+            pass_on(k - 1)
+
+        return carry
+
+    lax.fori_loop(0, half, step, 0)
+    pair(half - 1).wait_recv()
+    total = mine[half - 1] + first_recv[half - 1]
     for k in range(half - 1):
-        seconds[k].wait()
+        row(k).wait_recv()
         total = total + second_recv[k].astype(jnp.float32)
     rows = total.shape[0]
     shifted = (total + dual_ref[...]).reshape(rows // hours, hours, total.shape[1])
@@ -184,68 +226,75 @@
     clipped = jnp.minimum(jnp.maximum(shifted, -bound), bound)
     dual = (shifted - clipped).reshape(total.shape)
     own_ref[...] = dual
-    all_ref[spot, core] = dual.astype(jnp.bfloat16)
-
-    outs = []
-    for k, s in enumerate(spots):
-        outs.append(remote(
-            all_ref.at[spot, core], all_ref.at[spot, core], out_send.at[k], out_recv.at[k], s * 2 + core
-        ))
-    forwards = [remote(
-        all_ref.at[spot, core], all_ref.at[spot, core],
-        fwd_send.at[half - 1], fwd_recv.at[half - 1], partner,
-    )]
+    all_ref[me] = dual.astype(jnp.bfloat16)
+
+    far, lane = me // 4, lax.rem(me, 4)
+    across = me + 2 - 4 * lax.rem(me // 2, 2)
+    copies = []
+
+    def send(chunk, sends, recvs, k, device):
+        copy = remote(all_ref.at[chunk], all_ref.at[chunk], sends.at[k], recvs.at[k], device)
+        copy.start()
+        copies.append(copy)
+        return copy
+
+    fars = [
+        send(me, far_send, far_recv, k, lax.rem(far + k + 1, quarter) * 4 + lane) for k in range(quarter - 1)
+    ]
+    mids = [send(me, mid_send, mid_recv, 0, across)]
+    send(me, near_send, near_recv, 0, partner)
+    for k in range(quarter - 1):
+        fars[k].wait_recv()
+        source = lax.rem(far + quarter - k - 1, quarter) * 4
+        mids.append(send(source + lane, mid_send, mid_recv, k + 1, across))
+        send(source + lane, near_send, near_recv, k + 1, partner)
+    nears = copies[quarter:quarter + 1] + copies[quarter + 2::2]
+    for k in range(quarter):
+        mids[k].wait_recv()
+        source = lax.rem(far + quarter - k, quarter) * 4 + lax.rem(across, 4)
+        nears.append(send(source, near_send, near_recv, quarter + k, partner))
+    for copy in nears:
+        copy.wait_recv()
+    for copy in copies:
+        copy.wait_send()
+    for k in range(half):
+        pair(k).wait_send()
     for k in range(half - 1):
-        outs[k].wait_recv()
-        source = lax.rem(spot + half - k - 1, half)
-        forwards.append(remote(
-            all_ref.at[source, core], all_ref.at[source, core], fwd_send.at[k], fwd_recv.at[k], partner
-        ))
-    for copy in outs:
-        copy.wait_send()
-    for copy in forwards:
-        copy.wait()
-
-
-def clip_exchange(n, hours, flow, dual, limits, collective_id):
-    half = n // 2
+        row(k).wait_send()
+
+
+def flow_clip(n, tile_block, sent, dual, limits, tiles, collective_id):
+    half, quarter = n // 2, n // 4
+    hours = sent.shape[1]
+    own_groups = tiles.shape[0] // n
     chunk = dual.shape
+    slots = 4
     dma = pltpu.SemaphoreType.DMA
     return pl.pallas_call(
-        functools.partial(clip_kernel, n, hours),
+        functools.partial(flow_clip_kernel, n, hours),
         out_shape=(
-            jax.ShapeDtypeStruct((half, 2) + chunk, jnp.bfloat16),
+            jax.ShapeDtypeStruct((n,) + chunk, jnp.bfloat16),
             jax.ShapeDtypeStruct(chunk, jnp.float32),
         ),
-        in_specs=[VM] * 3,
+        in_specs=[pl.BlockSpec(memory_space=pltpu.SMEM)] + [VM] * 3 + [pl.BlockSpec(memory_space=pl.ANY)],
         out_specs=(VM, VM),
         scratch_shapes=[
+            pltpu.VMEM((slots, own_groups) + tiles.shape[1:], tiles.dtype),
+            pltpu.VMEM((half,) + chunk, jnp.float32),
+            pltpu.VMEM((half,) + chunk, jnp.float32),
             pltpu.VMEM((half,) + chunk, jnp.float32),
             pltpu.VMEM((half - 1,) + chunk, jnp.bfloat16),
             pltpu.VMEM((half - 1,) + chunk, jnp.bfloat16),
+            dma((slots,)),
             dma((half,)), dma((half,)),
             dma((half - 1,)), dma((half - 1,)),
-            dma((half - 1,)), dma((half - 1,)),
+            dma((quarter - 1,)), dma((quarter - 1,)),
+            dma((quarter,)), dma((quarter,)),
             dma((half,)), dma((half,)),
         ],
         compiler_params=pltpu.CompilerParams(collective_id=collective_id, has_side_effects=True),
-        name=f"clip_{collective_id}",
-    )(flow.reshape((half, 2) + chunk), dual, limits)
-
-
-def flow_kernel(block_ref, sent_ref, *refs):
-    step = pl.program_id(0)
-    tile_refs, out_ref = refs[:-1], refs[-1]
-    each, depth = tile_refs[0].shape[:2]
-    count = each * len(tile_refs)
-    for g in range(count):
-        picked = jnp.concatenate(
-            [sent_ref[block_ref[step * count + g, k]] for k in range(depth)], axis=1
-        )
-        wide = jnp.concatenate([tile_refs[g // each][g % each, k] for k in range(depth)], axis=1)
-        out_ref[g] = lax.dot_general(
-            picked, wide, (((1,), (1,)), ((), ())), preferred_element_type=jnp.float32
-        ).astype(out_ref.dtype)
+        name=f"flow_clip_{collective_id}",
+    )(tile_block, sent, dual, limits, tiles)
 
 
 def tile_specs(tiles, count):
@@ -254,25 +303,6 @@
         pl.BlockSpec(shape, lambda i, b, part=part: (i * STREAMS + part, 0, 0, 0))
         for part in range(STREAMS)
     ]
-
-
-def partial_flow(tile_block, sent, tiles, count):
-    groups, depth, lines, width = tiles.shape
-    blocks, hours = sent.shape[:2]
-    return pl.pallas_call(
-        flow_kernel,
-        out_shape=jax.ShapeDtypeStruct((groups, hours, lines), jnp.float32),
-        grid_spec=pltpu.PrefetchScalarGridSpec(
-            num_scalar_prefetch=1,
-            grid=(groups // count,),
-            in_specs=[
-                pl.BlockSpec((blocks, hours, width), lambda i, b: (0, 0, 0)),
-                *tile_specs(tiles, count),
-            ],
-            out_specs=pl.BlockSpec((count, hours, lines), lambda i, b: (i, 0, 0)),
-        ),
-        name="flow",
-    )(tile_block, sent, *([tiles] * STREAMS))
 
 
 def price_kernel(
@@ -409,8 +439,7 @@
     inj, sent = base, base
     dual = jnp.zeros((own_groups * hours, lines), jnp.float32)
     for iteration in range(ITERS):
-        flow = partial_flow(tile_block, sent, ptdf_tiles, count)
-        dual_all, dual = clip_exchange(n, hours, flow, dual, own_limits, 1 + iteration)
+        dual_all, dual = flow_clip(n, tile_block, sent, dual, own_limits, ptdf_tiles, 1 + iteration)
         inj, sent, level = price_update(
             iteration == ITERS - 1, tile_block, dual_all.reshape(groups, hours, lines), ptdf_tiles,
             base, inj, level, gain, unit_bus, count,

time: 137 us -> 120 us (0.88); the launches traced: 137 us -> 118 us
  Pallas kernels: 125 us -> 106 us
    pallas_call x4 -> x2, Pallas kernels: 72.3 us -> 56 us  [flow_clip(): pl.pallas_call(functools.partial(flow_clip_kernel, n, hours), out_shape=(...]
    pallas_call x1, Pallas kernels: 12.7 us -> 10.3 us  [closing(): pl.pallas_call(functools.partial(closing_kernel, n), out_shape=(jax.Shape...]
where the time goes in v3:
time: 120 us; the launch traced here: 118 us
  Pallas kernels  106 us (88%)
  local copies, waits for them, and re-layouts  10.1 us (8%)
  other arithmetic  1.31 us (1%)
    pallas_call x2, Pallas kernels, flow_clip(): pl.pallas_call(functools.partial(flow_clip_kernel, n, hours), out_shape=(...  56 us
    pallas_call x2, Pallas kernels, price_update(): pl.pallas_call(functools.partial(price_kernel, chunk, last, depth), out_s...  26.6 us
    pallas_call x1, Pallas kernels, opening(): pl.pallas_call(functools.partial(opening_kernel, n), out_shape=(jax.Shape...  13.2 us
    pallas_call x1, Pallas kernels, closing(): pl.pallas_call(functools.partial(closing_kernel, n), out_shape=(jax.Shape...  10.3 us
    unnamed x7, local copies, waits for them, and re-layouts  8.2 us

profile of v3, /device:TPU:0, one launch (start us, length us, event | category | flops | bytes accessed | tf_op | source)
XLA Modules:
  0.0 118.1 jit_solution(1931978490566230028)
XLA Ops:
  0.6 0.0 copy-start
  0.6 0.8 copy-done
  1.5 0.6 constant_dynamic-slice_fusion.limits_ref
  2.1 1.4 %copy.18.block_ref = s32[128,5]{1,0:T(8,128)} copy(s32[128,5]{0,1:T(8,128)} %param.9) | data formatting | bytes 5120 | tf_op args[2]
  3.5 13.2 %opening.1 = (bf16[16,1,2304]{2,1,0:T(2,128)(2,1)}, f32[16,1,2048]{2,1,0:T(1,128)}) custom-call(bf16[1,36864]{1,0:T(2,128)(2,1)} %base_ref.1, f32[1,2048]{1,0:T(1,128)} %soc_ref.1), custom_call_target="tpu_custom_call" | custom-call | tf_op jit(solution)/shard_map/opening/pallas_call | solution.py:57
  16.7 1.3 %reduce = bf16[16,2304]{1,0:T(8,128)(2,1)S(1)} reduce(bf16[16,1,2304]{2,1,0:T(2,128)(2,1)} %get-tuple-element.14, bf16[]{:T(256)} %constant.16), dimensions={1}, to_apply=%get-tuple-element.14.reduce_sub_computation | reduce | bytes 147458 | tf_op jit(solution)/shard_map/opening/pallas_call | solution.py:57
  18.0 0.6 bitcast_bitcast_fusion.sent_ref.refs_4_.refs_5_
  18.7 1.6 %copy.23 = f32[16,1,2048]{2,0,1:T(8,128)} copy(f32[16,1,2048]{2,1,0:T(1,128)} %get-tuple-element.16) | data formatting | bytes 262144
  20.3 0.6 broadcast_in_dim.3.dual_ref
  20.9 30.1 %flow_clip_1.1 = (bf16[16,128,128]{2,1,0:T(8,128)(2,1)}, f32[128,128]{1,0:T(8,128)}) custom-call(s32[128,5]{1,0:T(8,128)} %copy.18.block_ref, bf16[18,16,128]{2,1,0:T(8,128)(2,1)} %bitcast_bitcast_fusion.sent_ref.refs_4_.refs_5_, f32[128,128]{1,0:T(8,128)} %broadcast_in_dim.3.dual_ref, f32[8,128]{1,0:T(8,128)} %constant_dynamic-slice_fusion.limits_ref, ...), custom_call_target="tpu_custom_call" | custom-call | tf_op jit(solution)/shard_map/flow_clip_1/pallas_call | solution.py:273
  51.0 13.6 %price.2 = (f32[18,16,128]{2,1,0:T(8,128)}, bf16[18,16,128]{2,1,0:T(8,128)(2,1)}, f32[16,2048]{1,0:T(8,128)}) custom-call(s32[128,5]{1,0:T(8,128)} %copy.18.block_ref, bf16[128,16,128]{2,1,0:T(8,128)(2,1)} %bitcast.17, bf16[128,5,128,128]{3,2,1,0:T(8,128)(2,1)} %refs_3_.3, bf16[128,5,128,128]{3,2,1,0:T(8,128)(2,1)} %refs_3_.3, ...), custom_call_target="tpu_custom_call" | custom-call | tf_op jit(solution)/shard_map/price/pallas_call | solution.py:401
  64.6 25.9 %flow_clip_2.1 = (bf16[16,128,128]{2,1,0:T(8,128)(2,1)}, f32[128,128]{1,0:T(8,128)}) custom-call(s32[128,5]{1,0:T(8,128)} %copy.18.block_ref, bf16[18,16,128]{2,1,0:T(8,128)(2,1)} %get-tuple-element.17.sent_ref, f32[128,128]{1,0:T(8,128)} %get-tuple-element.18.dual_ref, f32[8,128]{1,0:T(8,128)} %constant_dynamic-slice_fusion.limits_ref, ...), custom_call_target="tpu_custom_call" | custom-call | tf_op jit(solution)/shard_map/flow_clip_2/pallas_call | solution.py:273
  90.5 13.0 %price.3 = (f32[16,1,2304]{2,1,0:T(1,128)}, f32[8,128]{1,0:T(8,128)}, f32[16,16,128]{2,1,0:T(8,128)}) custom-call(s32[128,5]{1,0:T(8,128)} %copy.18.block_ref, bf16[128,16,128]{2,1,0:T(8,128)(2,1)} %bitcast.16, bf16[128,5,128,128]{3,2,1,0:T(8,128)(2,1)} %refs_3_.3, bf16[128,5,128,128]{3,2,1,0:T(8,128)(2,1)} %refs_3_.3, bf16[128,5,128,128]{3,2,1,0:T(8,128)(2,1)} %refs_3_.3, ...), custom_call_target="tpu_custom_call" | custom-call | tf_op jit(solution)/shard_map/price/pallas_call | solution.py:401
  103.5 10.3 %closing.1 = (f32[1,36864]{1,0:T(1,128)}, f32[1,16384]{1,0:T(1,128)}, f32[1,2048]{1,0:T(1,128)}) custom-call(f32[16,1,2304]{2,1,0:T(1,128)} %get-tuple-element.22.inj_ref, f32[128,128]{1,0:T(8,128)} %get-tuple-element.23.dual_ref, f32[16,16,128]{2,1,0:T(8,128)} %get-tuple-element.24.level_ref), custom_call_target="tpu_custom_call" | custom-call | tf_op jit(solution)/shard_map/closing/pallas_call | solution.py:120
  113.7 1.6 %copy.27 = f32[1,36864]{1,0:T(1,128)} copy(f32[1,36864]{1,0:T(1,128)} %get-tuple-element.28) | data formatting | bytes 294912
  115.3 1.5 %copy.28 = f32[1,16384]{1,0:T(1,128)} copy(f32[1,16384]{1,0:T(1,128)} %get-tuple-element.29) | data formatting | bytes 131072
  116.8 1.3 %copy.29 = f32[1,2048]{1,0:T(1,128)} copy(f32[1,2048]{1,0:T(1,128)} %get-tuple-element.30) | data formatting | bytes 16384
Async XLA Ops:
  0.6 0.8 copy-start

commit v4 on v3

--- a/solution.py
+++ b/solution.py
@@ -29,46 +29,51 @@
     pl.semaphore_wait(barrier, len(others))
 
 
-def opening_kernel(n, base_ref, soc_ref, base_out, soc_out, send_sem, recv_sem):
+def opening_kernel(n, base_ref, out_ref, rows, wide, send_sem, recv_sem):
     me = lax.axis_index("tm")
-    width = base_out.shape[2]
+    reach = rows.shape[2]
+    blocks, _, width = out_ref.shape
     others = [lax.rem(me + k, n) for k in range(1, n)]
     greet(others)
     copies = []
     for k, other in enumerate(others):
-        for part, (src, dst) in enumerate((
-            (base_ref.at[:, pl.ds(pl.multiple_of(other * width, width), width)], base_out.at[me]),
-            (soc_ref, soc_out.at[me]),
-        )):
-            copy = pltpu.make_async_remote_copy(
-                src_ref=src, dst_ref=dst,
-                send_sem=send_sem.at[part, k], recv_sem=recv_sem.at[part, k],
-                device_id=peer(other), device_id_type=MESH,
-            )
-            copy.start()
-            copies.append(copy)
-    base_out[me] = base_ref[:, pl.ds(pl.multiple_of(me * width, width), width)]
-    soc_out[me] = soc_ref[...]
+        copy = pltpu.make_async_remote_copy(
+            src_ref=base_ref.at[:, pl.ds(pl.multiple_of(other * reach, reach), reach)],
+            dst_ref=rows.at[me],
+            send_sem=send_sem.at[k],
+            recv_sem=recv_sem.at[k],
+            device_id=peer(other),
+            device_id_type=MESH,
+        )
+        copy.start()
+        copies.append(copy)
+    rows[me] = base_ref[:, pl.ds(pl.multiple_of(me * reach, reach), reach)]
     for copy in copies:
         copy.wait()
-
-
-def opening(n, base, soc):
+    for h in range(n):
+        row = rows[h].astype(jnp.float32)
+        for b in range(blocks):
+            wide[b, h:h + 1, :] = row[:, b * width:(b + 1) * width]
+    out_ref[...] = wide[...].astype(out_ref.dtype)
+
+
+def opening(n, base, width):
+    reach = base.shape[1] // n
+    shape = (reach // width, n, width)
     return pl.pallas_call(
         functools.partial(opening_kernel, n),
-        out_shape=(
-            jax.ShapeDtypeStruct((n, 1, base.shape[1] // n), base.dtype),
-            jax.ShapeDtypeStruct((n,) + soc.shape, soc.dtype),
-        ),
-        in_specs=[VM] * 2,
-        out_specs=(VM, VM),
+        out_shape=jax.ShapeDtypeStruct(shape, base.dtype),
+        in_specs=[VM],
+        out_specs=VM,
         scratch_shapes=[
-            pltpu.SemaphoreType.DMA((2, n - 1)),
-            pltpu.SemaphoreType.DMA((2, n - 1)),
+            pltpu.VMEM((n, 1, reach), base.dtype),
+            pltpu.VMEM(shape, jnp.float32),
+            pltpu.SemaphoreType.DMA((n - 1,)),
+            pltpu.SemaphoreType.DMA((n - 1,)),
         ],
         compiler_params=pltpu.CompilerParams(collective_id=0, has_side_effects=True),
         name="opening",
-    )(base, soc)
+    )(base)
 
 
 def closing_kernel(
@@ -139,11 +144,16 @@
 
 
 def flow_clip_kernel(
-    n, hours, block_ref, sent_ref, dual_ref, limits_ref, tiles_ref, all_ref, own_ref,
-    held, theirs, mine, first_recv, first_sum, second_recv,
-    tile_sem, pair_send, pair_recv, row_send, row_recv,
-    far_send, far_recv, mid_send, mid_recv, near_send, near_recv,
+    n, hours, opens, block_ref, sent_ref, extra_ref, limits_ref, tiles_ref, all_ref, own_ref, *refs
 ):
+    if opens:
+        level_ref, *refs = refs
+        *refs, level_recv, level_send_sem, level_recv_sem = refs
+    (
+        held, theirs, mine, first_recv, first_sum, second_recv,
+        tile_sem, pair_send, pair_recv, row_send, row_recv,
+        far_send, far_recv, mid_send, mid_recv, near_send, near_recv,
+    ) = refs
     half, quarter = n // 2, n // 4
     me = lax.axis_index("tm")
     core = lax.rem(me, 2)
@@ -188,7 +198,17 @@
     for k in range(ahead):
         fetch(k, True, 2 * k).start()
         fetch(k, False, 2 * k + 1).start()
-    greet([partner] + [s * 2 + core for s in spots])
+    levels = []
+    if opens:
+        everyone = [lax.rem(me + k, n) for k in range(1, n)]
+        greet(everyone)
+        for k, other in enumerate(everyone):
+            copy = remote(extra_ref, level_recv.at[me], level_send_sem.at[k], level_recv_sem.at[k], other)
+            copy.start()
+            levels.append(copy)
+        level_recv[me] = extra_ref[...]
+    else:
+        greet([partner] + [s * 2 + core for s in spots])
 
     def pass_on(k):
         pair(k).wait_recv()
@@ -221,8 +241,10 @@
         row(k).wait_recv()
         total = total + second_recv[k].astype(jnp.float32)
     rows = total.shape[0]
-    shifted = (total + dual_ref[...]).reshape(rows // hours, hours, total.shape[1])
-    bound = limits_ref[...][:, None, :]
+    if not opens:
+        total = total + extra_ref[...]
+    shifted = total.reshape(rows // hours, hours, total.shape[1])
+    bound = limits_ref[pl.ds(me * own_groups, own_groups), :][:, None, :]
     clipped = jnp.minimum(jnp.maximum(shifted, -bound), bound)
     dual = (shifted - clipped).reshape(total.shape)
     own_ref[...] = dual
@@ -253,6 +275,11 @@
         mids[k].wait_recv()
         source = lax.rem(far + quarter - k, quarter) * 4 + lax.rem(across, 4)
         nears.append(send(source, near_send, near_recv, quarter + k, partner))
+    if opens:
+        for copy in levels:
+            copy.wait()
+        for h in range(n):
+            level_ref[h:h + 1, :] = level_recv[h]
     for copy in nears:
         copy.wait_recv()
     for copy in copies:
@@ -263,21 +290,26 @@
         row(k).wait_send()
 
 
-def flow_clip(n, tile_block, sent, dual, limits, tiles, collective_id):
+def flow_clip(n, tile_block, sent, extra, limits, tiles, opens, collective_id):
     half, quarter = n // 2, n // 4
     hours = sent.shape[1]
     own_groups = tiles.shape[0] // n
-    chunk = dual.shape
+    chunk = (own_groups * hours, tiles.shape[2])
     slots = 4
     dma = pltpu.SemaphoreType.DMA
+    outs = [
+        jax.ShapeDtypeStruct((n,) + chunk, jnp.bfloat16),
+        jax.ShapeDtypeStruct(chunk, jnp.float32),
+    ]
+    more = []
+    if opens:
+        outs.append(jax.ShapeDtypeStruct((n, extra.shape[1]), extra.dtype))
+        more = [pltpu.VMEM((n,) + extra.shape, extra.dtype), dma((n - 1,)), dma((n - 1,))]
     return pl.pallas_call(
-        functools.partial(flow_clip_kernel, n, hours),
-        out_shape=(
-            jax.ShapeDtypeStruct((n,) + chunk, jnp.bfloat16),
-            jax.ShapeDtypeStruct(chunk, jnp.float32),
-        ),
+        functools.partial(flow_clip_kernel, n, hours, opens),
+        out_shape=tuple(outs),
         in_specs=[pl.BlockSpec(memory_space=pltpu.SMEM)] + [VM] * 3 + [pl.BlockSpec(memory_space=pl.ANY)],
-        out_specs=(VM, VM),
+        out_specs=(VM,) * len(outs),
         scratch_shapes=[
             pltpu.VMEM((slots, own_groups) + tiles.shape[1:], tiles.dtype),
             pltpu.VMEM((half,) + chunk, jnp.float32),
@@ -291,10 +323,10 @@
             dma((quarter - 1,)), dma((quarter - 1,)),
             dma((quarter,)), dma((quarter,)),
             dma((half,)), dma((half,)),
-        ],
+        ] + more,
         compiler_params=pltpu.CompilerParams(collective_id=collective_id, has_side_effects=True),
         name=f"flow_clip_{collective_id}",
-    )(tile_block, sent, dual, limits, tiles)
+    )(tile_block, sent, extra, limits, tiles)
 
 
 def tile_specs(tiles, count):
@@ -420,26 +452,24 @@
 
 def shards(base_injection, ptdf_tiles, tile_block, limits, stor_bus, stor_gain, soc_init):
     n = lax.axis_size("tm")
-    me = lax.axis_index("tm")
     hours = n * base_injection.shape[0]
     groups, _, lines, width = ptdf_tiles.shape
     units = soc_init.shape[1]
-    blocks = base_injection.shape[1] // (n * width)
-    own_groups = groups // n
     count = 32
 
-    base, level = opening(n, base_injection, soc_init)
-    base = jnp.transpose(base.reshape(hours, blocks, width), (1, 0, 2))
-    level = level.reshape(hours, units)
-
+    base = opening(n, base_injection, width)
     unit_bus = stor_bus.reshape(1, units)
     gain = stor_gain.reshape(1, units)
-    own_limits = lax.dynamic_slice_in_dim(limits.reshape(groups, lines), me * own_groups, own_groups, 0)
+    bounds = limits.reshape(groups, lines)
 
     inj, sent = base, base
-    dual = jnp.zeros((own_groups * hours, lines), jnp.float32)
     for iteration in range(ITERS):
-        dual_all, dual = flow_clip(n, tile_block, sent, dual, own_limits, ptdf_tiles, 1 + iteration)
+        opens = iteration == 0
+        dual_all, dual, *gathered = flow_clip(
+            n, tile_block, sent, soc_init if opens else dual, bounds, ptdf_tiles, opens, 1 + iteration
+        )
+        if opens:
+            level, = gathered
         inj, sent, level = price_update(
             iteration == ITERS - 1, tile_block, dual_all.reshape(groups, hours, lines), ptdf_tiles,
             base, inj, level, gain, unit_bus, count,

time: 120 us -> 111 us (0.925)
  local copies, waits for them, and re-layouts: 10.1 us -> 5.77 us
  Pallas kernels: 106 us -> 103 us
  other arithmetic: 1.31 us -> 0 us
    pallas_call x3, Pallas kernels: 69.2 us -> 66.6 us  [the longest x2 55.6 us: flow_clip(): pl.pallas_call(functools.partial(flow_clip_kernel, n, hours, opens), out_...]
    unnamed x7 -> x4, local copies, waits for them, and re-layouts: 8.2 us -> 5.77 us
    pallas_call x1 -> x0, other arithmetic: 1.31 us -> none  [opening(): pl.pallas_call(functools.partial(opening_kernel, n), out_shape=(jax.Shape...]
where the time goes in v4:
time: 111 us; the launch traced here: 110 us
  Pallas kernels  103 us (93%)
  local copies, waits for them, and re-layouts  5.77 us (5%)
    pallas_call x2, Pallas kernels, flow_clip(): pl.pallas_call(functools.partial(flow_clip_kernel, n, hours, opens), out_...  55.6 us
    pallas_call x2, Pallas kernels, price_update(): pl.pallas_call(functools.partial(price_kernel, chunk, last, depth), out_s...  26.6 us
    pallas_call x1, Pallas kernels, opening(): pl.pallas_call(functools.partial(opening_kernel, n), out_shape=jax.ShapeD...  11 us
    pallas_call x1, Pallas kernels, closing(): pl.pallas_call(functools.partial(closing_kernel, n), out_shape=(jax.Shape...  10.2 us
    unnamed x4, local copies, waits for them, and re-layouts  5.77 us

profile of v4, /device:TPU:0, one launch (start us, length us, event | category | flops | bytes accessed | tf_op | source)
XLA Modules:
  0.0 109.9 jit_solution(17550420949109246808)
XLA Ops:
  0.6 1.4 %copy.13.block_ref = s32[128,5]{1,0:T(8,128)} copy(s32[128,5]{0,1:T(8,128)} %param.9) | data formatting | bytes 5120 | tf_op args[2]
  2.1 11.0 %opening.1.sent_ref.refs_4_.refs_5_ = bf16[18,16,128]{2,1,0:T(8,128)(2,1)} custom-call(bf16[1,36864]{1,0:T(2,128)(2,1)} %base_ref.1), custom_call_target="tpu_custom_call" | custom-call | tf_op jit(solution)/shard_map/opening/pallas_call | solution.py:63
  13.0 29.7 %flow_clip_1.1 = (bf16[16,128,128]{2,1,0:T(8,128)(2,1)}, f32[128,128]{1,0:T(8,128)}, f32[16,2048]{1,0:T(8,128)}) custom-call(s32[128,5]{1,0:T(8,128)} %copy.13.block_ref, bf16[18,16,128]{2,1,0:T(8,128)(2,1)} %opening.1.sent_ref.refs_4_.refs_5_, f32[1,2048]{1,0:T(1,128)} %extra_ref.1, f32[128,128]{1,0:T(8,128)} %bitcast.7, bf16[128,5,128,128]{3,2,1,0:T(8,128)(2,1)} %refs_3_.3), custom_call_target="tpu_custom_call" | custom-call | tf_op jit(solution)/shard_map/flow_clip_1/pallas_call | solution.py:308
  42.8 13.6 %price.2 = (f32[18,16,128]{2,1,0:T(8,128)}, bf16[18,16,128]{2,1,0:T(8,128)(2,1)}, f32[16,2048]{1,0:T(8,128)}) custom-call(s32[128,5]{1,0:T(8,128)} %copy.13.block_ref, bf16[128,16,128]{2,1,0:T(8,128)(2,1)} %bitcast.6, bf16[128,5,128,128]{3,2,1,0:T(8,128)(2,1)} %refs_3_.3, bf16[128,5,128,128]{3,2,1,0:T(8,128)(2,1)} %refs_3_.3, ...), custom_call_target="tpu_custom_call" | custom-call | tf_op jit(solution)/shard_map/price/pallas_call | solution.py:433
  56.4 25.9 %flow_clip_2.1 = (bf16[16,128,128]{2,1,0:T(8,128)(2,1)}, f32[128,128]{1,0:T(8,128)}) custom-call(s32[128,5]{1,0:T(8,128)} %copy.13.block_ref, bf16[18,16,128]{2,1,0:T(8,128)(2,1)} %get-tuple-element.15.sent_ref, f32[128,128]{1,0:T(8,128)} %get-tuple-element.16.extra_ref, f32[128,128]{1,0:T(8,128)} %bitcast.8, bf16[128,5,128,128]{3,2,1,0:T(8,128)(2,1)} %refs_3_.3), custom_call_target="tpu_custom_call" | custom-call | tf_op jit(solution)/shard_map/flow_clip_2/pallas_call | solution.py:308
  82.3 13.0 %price.3 = (f32[16,1,2304]{2,1,0:T(1,128)}, f32[8,128]{1,0:T(8,128)}, f32[16,16,128]{2,1,0:T(8,128)}) custom-call(s32[128,5]{1,0:T(8,128)} %copy.13.block_ref, bf16[128,16,128]{2,1,0:T(8,128)(2,1)} %bitcast.5, bf16[128,5,128,128]{3,2,1,0:T(8,128)(2,1)} %refs_3_.3, bf16[128,5,128,128]{3,2,1,0:T(8,128)(2,1)} %refs_3_.3, bf16[128,5,128,128]{3,2,1,0:T(8,128)(2,1)} %refs_3_.3, ...), custom_call_target="tpu_custom_call" | custom-call | tf_op jit(solution)/shard_map/price/pallas_call | solution.py:433
  95.3 10.2 %closing.1 = (f32[1,36864]{1,0:T(1,128)}, f32[1,16384]{1,0:T(1,128)}, f32[1,2048]{1,0:T(1,128)}) custom-call(f32[16,1,2304]{2,1,0:T(1,128)} %get-tuple-element.20.inj_ref, f32[128,128]{1,0:T(8,128)} %get-tuple-element.21.dual_ref, f32[16,16,128]{2,1,0:T(8,128)} %get-tuple-element.22.level_ref), custom_call_target="tpu_custom_call" | custom-call | tf_op jit(solution)/shard_map/closing/pallas_call | solution.py:125
  105.5 1.6 %copy.17 = f32[1,36864]{1,0:T(1,128)} copy(f32[1,36864]{1,0:T(1,128)} %get-tuple-element.26) | data formatting | bytes 294912
  107.1 1.5 %copy.18 = f32[1,16384]{1,0:T(1,128)} copy(f32[1,16384]{1,0:T(1,128)} %get-tuple-element.27) | data formatting | bytes 131072
  108.6 1.3 %copy.19 = f32[1,2048]{1,0:T(1,128)} copy(f32[1,2048]{1,0:T(1,128)} %get-tuple-element.28) | data formatting | bytes 16384
